TPU v7x, 32 devices: a whole 2x2x4 slice. The times are simulated.
32 devices in a mesh: fsdp: 8 (over z, x), tp: 4 (over y, core).
Axes of the slice: x: 2, y: 2, z: 4, core: 2. Of those that a mesh axis runs over, the one named last changes fastest.
Arguments:
- inputs: float32 [16384, 768], P(('fsdp', 'tp')), may hold values from -6 to 6
- cotangent: float32 [16384, 768], P(('fsdp', 'tp')), may hold values from -6 to 6
- lengths: int32 [8, 4], P('fsdp'), may hold values from 1 to 768, as said below
- routes: int32 [16384, 2], P('fsdp'), may hold values from 0 to 11, all different within a row
- drop_order: int32 [16384, 2], P('fsdp'), may hold values from 0 to 4095, as said below
- prior_logits: float32 [16384, 12], P('fsdp'), may hold values from -6 to 6
- attn_gain: float32 [768], replicated, may hold values from 0.5 to 1.5
- w_query: bfloat16 [768, 768], P('fsdp', 'tp'), may hold values from -0.21875 to 0.21875
- w_key: bfloat16 [768, 768], P('fsdp', 'tp'), may hold values from -0.21875 to 0.21875
- w_value: bfloat16 [768, 768], P('fsdp', 'tp'), may hold values from -0.21875 to 0.21875
- w_out: bfloat16 [768, 768], P('tp', 'fsdp'), may hold values from -3.5 to 3.5
- moe_gain: float32 [768], replicated, may hold values from 0.5 to 1.5
- w_router: float32 [768, 12], replicated, may hold values from -0.21875 to 0.21875
- w_prior: float32 [12, 12], replicated, may hold values from -1.75 to 1.75
- w_const: float32 [2, 768, 2], replicated, may hold values from -0.21875 to 0.21875
- const_vector: float32 [2, 768], replicated, may hold values from -6 to 6
- w_gate: bfloat16 [8, 768, 2048], P(None, 'fsdp', 'tp'), may hold values from -0.21875 to 0.21875
- w_up: bfloat16 [8, 768, 2048], P(None, 'fsdp', 'tp'), may hold values from -0.21875 to 0.21875
- w_down: bfloat16 [8, 2048, 768], P(None, 'tp', 'fsdp'), may hold values from -2 to 2
Outputs:
- output: float32 [16384, 768], P(('fsdp', 'tp'))
- grad_inputs: float32 [16384, 768], P(('fsdp', 'tp'))
- grad_prior: float32 [16384, 12], P(('fsdp', 'tp'))
- grad_attn_gain: float32 [768], replicated
- grad_w_query: float32 [768, 768], P('fsdp', 'tp')
- grad_w_key: float32 [768, 768], P('fsdp', 'tp')
- grad_w_value: float32 [768, 768], P('fsdp', 'tp')
- grad_w_out: float32 [768, 768], P('tp', 'fsdp')
- grad_moe_gain: float32 [768], replicated
- grad_w_router: float32 [768, 12], replicated
- grad_w_prior: float32 [12, 12], replicated
- grad_w_const: float32 [2, 768, 2], replicated
- grad_const_vector: float32 [2, 768], replicated
- grad_w_gate: float32 [8, 768, 2048], P(None, 'fsdp', 'tp')
- grad_w_up: float32 [8, 768, 2048], P(None, 'fsdp', 'tp')
- grad_w_down: float32 [8, 2048, 768], P(None, 'tp', 'fsdp')
Inputs may be any that keep to these rules, and one draw needn't show every extreme that they name: In each row the first 3 entries are the group's sequence lengths in order and the last counts padding tokens at the group's end; each row sums to 2048. Every sequence has 512 tokens or more, one sequence of each row has exactly 768, and the padding is 1 or more. `routes`: each token names two different experts: 0 to 7 feed-forward, 8 zero, 9 copy, 10 and 11 constant. `drop_order`: within each group the 4096 pairs carry each rank once.
All inputs are finite; a program needn't handle non-finite values.
Results may differ from a plain program's by a relative error of at most 0.015.
Values may be sent and summed in bfloat16 or wider, within the bound.
No kernel may reach another device: no remote copies, remote signals or barrier semaphores. Data moves between devices by JAX's collectives and lax.ppermute only.
A program may use at most 256 MiB of HBM per device.

v0:
```python
import functools

import jax
import jax.numpy as jnp
from jax import lax
from jax.experimental import pallas as pl
from jax.experimental.pallas import tpu as pltpu
from jax.sharding import Mesh
from jax.sharding import PartitionSpec as P

HEAD = 64
MAXLEN = 768
LOW = 4
SHARDS = 8
LOW_PLACE = 4
BOUNDS = 5
EPSILON = 1e-06
PRECISE = lax.Precision.HIGHEST
NEGATIVE = -1e30
F32 = jnp.float32
BF16 = jnp.bfloat16


def rms_norm(values, gain):
    return values * lax.rsqrt(jnp.mean(values * values, axis=-1, keepdims=True) + EPSILON) * gain


def swap(value, axis):
    return lax.ppermute(value, axis, [(0, 1), (1, 0)])


def gather_pieces(value):
    other = swap(value, "y")
    return [value, swap(value, "c"), other, swap(other, "c")]


def natural(pieces, index):
    ordered = []
    for j in range(4):
        item = pieces[j]
        for t in range(1, 4):
            item = jnp.where(index == t, pieces[j ^ t], item)
        ordered.append(item)
    return jnp.stack(ordered)


def add_core(near, sent):
    got = swap(sent, "c")
    return got, (near[1] + got[1].astype(F32)).astype(BF16)


def cost_of(microseconds):
    return pl.CostEstimate(
        flops=int(microseconds * 1.15e9), transcendentals=0, bytes_accessed=2**16
    )


def start_of(row, scalars):
    start_row = jnp.zeros_like(row)
    for k in range(BOUNDS, scalars.shape[0]):
        start_row = jnp.where(row >= scalars[k], scalars[k], start_row)
    return start_row


def for_window(first, block, pad, scalars, body):
    needed = (first - start_of(first, scalars) + block - 1) // block
    most = pad // block
    for blocks in range(most):
        pl.when(needed == blocks)(functools.partial(body, (blocks + 1) * block))
    pl.when(needed >= most)(functools.partial(body, pad + block))


def scores_mask(first_key, first_query, window, block, scalars):
    row = first_query + lax.broadcasted_iota(jnp.int32, (1, block), 1)
    start_row = start_of(row, scalars)
    key_places = first_key + lax.broadcasted_iota(jnp.int32, (window, block), 0)
    query_places = first_query + lax.broadcasted_iota(jnp.int32, (window, block), 1)
    return (key_places >= start_row) & (key_places <= query_places)


def attend_kernel(block, pad, scalars, *refs):
    pieces, refs = refs[:4], refs[4:]
    shards, refs = refs[:LOW], refs[LOW:]
    out_ref, lse_ref, qkv_ref, weight_ref, key_rows, value_pad, full = refs
    group = qkv_ref.shape[1]
    quarter = group // 4
    inner = qkv_ref.shape[0] // 3
    head = pl.program_id(0)

    @pl.when(head == 0)
    def _():
        rows = shards[0].shape[1]
        for r in range(SHARDS):
            place = pl.multiple_of((scalars[0] ^ r) * rows, rows)
            full[pl.ds(place, rows), :] = shards[r % LOW][r // LOW]
        turned = full[:, : 3 * inner].T
        weight_ref[...] = turned
        for r in range(4):
            place = pl.multiple_of((scalars[1] ^ r) * quarter, quarter)
            qkv_ref[:, pl.ds(place, quarter)] = lax.dot_general(
                turned, pieces[r][...], (((1,), (1,)), ((), ())), preferred_element_type=F32
            ).astype(BF16)

    first_row = pl.multiple_of(head * HEAD, HEAD)
    key_rows[pl.ds(0, pad), :] = jnp.zeros((pad, HEAD), BF16)
    value_pad[:, pl.ds(0, pad)] = jnp.zeros((HEAD, pad), BF16)
    key_rows[pl.ds(pad, group), :] = qkv_ref[pl.ds(inner + first_row, HEAD), :].T
    value_pad[:, pl.ds(pad, group)] = qkv_ref[pl.ds(2 * inner + first_row, HEAD), :]

    def one(i, carry):
        first = pl.multiple_of(i * block, block)

        def body(window):
            begin = pl.multiple_of(first + pad + block - window, block)
            scores = jnp.dot(
                key_rows[pl.ds(begin, window), :],
                qkv_ref[pl.ds(first_row, HEAD), pl.ds(first, block)],
                preferred_element_type=F32,
            )
            allowed = scores_mask(begin - pad, first, window, block, scalars)
            scores = jnp.where(allowed, scores * 0.125, NEGATIVE)
            highest = jnp.max(scores, axis=0, keepdims=True)
            weights = jnp.exp(scores - highest)
            total = jnp.sum(weights, axis=0, keepdims=True)
            mixed = jnp.dot(
                value_pad[:, pl.ds(begin, window)],
                weights.astype(BF16),
                preferred_element_type=F32,
            )
            mixed = (mixed / total).astype(BF16)
            column = pl.multiple_of(first % quarter, block)
            out_ref[first // quarter, :, pl.ds(column, block)] = mixed
            lse_ref[0, :, pl.ds(first, block)] = highest + jnp.log(total)

        for_window(first, block, pad, scalars, body)
        return carry

    lax.fori_loop(0, group // block, one, 0)


def attend(pieces, shards, scalars, heads):
    rows, width = pieces[0].shape
    group = 4 * rows
    inner = heads * HEAD
    block = 256

    def whole(shape):
        return pl.BlockSpec(
            shape, lambda i, _: (0,) * len(shape), pipeline_mode=pl.Buffered(1)
        )

    return pl.pallas_call(
        functools.partial(attend_kernel, block, MAXLEN),
        grid_spec=pltpu.PrefetchScalarGridSpec(
            num_scalar_prefetch=1,
            grid=(heads,),
            in_specs=[
                *[whole((rows, width)) for _ in range(4)],
                *[whole(shards[0].shape) for _ in range(LOW)],
            ],
            out_specs=[
                pl.BlockSpec((4, HEAD, rows), lambda h, _: (0, h, 0)),
                pl.BlockSpec((1, 1, group), lambda h, _: (h, 0, 0)),
                whole((3 * inner, group)),
                whole((3 * inner, width)),
            ],
            scratch_shapes=[
                pltpu.VMEM((MAXLEN + group, HEAD), BF16),
                pltpu.VMEM((HEAD, MAXLEN + group), BF16),
                pltpu.VMEM((width, 4 * inner), BF16),
            ],
        ),
        out_shape=[
            jax.ShapeDtypeStruct((4, inner, rows), BF16),
            jax.ShapeDtypeStruct((heads, 1, group), F32),
            jax.ShapeDtypeStruct((3 * inner, group), BF16),
            jax.ShapeDtypeStruct((3 * inner, width), BF16),
        ],
        compiler_params=pltpu.CompilerParams(vmem_limit_bytes=48 * 2**20),
        cost_estimate=cost_of(24),
        name="attend",
    )(scalars, *pieces, *shards)


def attn_grads_kernel(scalars, *refs):
    grad_qkv, mixed, refs = refs[0], refs[1], refs[2:]
    tokens, grads, refs = refs[:4], refs[4:8], refs[8:]
    outs, (total,) = refs[:2], refs[2:]
    inner3 = grad_qkv.shape[1]
    first, second = 0.0, 0.0
    for r in range(4):
        j = scalars[1] ^ r
        first += jnp.dot(grad_qkv[r], tokens[r][...], preferred_element_type=F32)
        second += jnp.dot(mixed[j], grads[r][...], preferred_element_type=F32)
    total[:, :inner3] = first.T.astype(BF16)
    total[:, inner3:] = second.T.astype(BF16)
    rows = outs[0].shape[1]
    for r in range(SHARDS):
        place = pl.multiple_of((scalars[0] ^ r) * rows, rows)
        outs[r // LOW][r % LOW] = total[pl.ds(place, rows), :]


def attn_grads(grad_qkv, mixed, tokens, grads, scalars):
    width = tokens[0].shape[1]
    columns = grad_qkv.shape[1] + mixed.shape[1]
    rows = width // SHARDS
    whole = pl.BlockSpec(memory_space=pltpu.VMEM)
    return pl.pallas_call(
        attn_grads_kernel,
        in_specs=[pl.BlockSpec(memory_space=pltpu.SMEM)] + [whole] * 10,
        out_specs=[whole] * 2,
        out_shape=[jax.ShapeDtypeStruct((LOW, rows, columns), BF16)] * 2,
        scratch_shapes=[pltpu.VMEM((width, columns), BF16)],
        compiler_params=pltpu.CompilerParams(vmem_limit_bytes=48 * 2**20),
        cost_estimate=cost_of(30),
        name="attn_grads",
    )(scalars, grad_qkv, mixed, *tokens, *grads)


def attend_back_kernel(block, pad, scalars, qkv_ref, lse_ref, *refs):
    pieces, refs = refs[:4], refs[4:]
    out_ref, grad_mixed, key_rows, value_rows, key_pad, grad_key, grad_value = refs
    group = qkv_ref.shape[1]
    inner_rows = qkv_ref.shape[0] // 3
    quarter = group // 4
    contract_last = (((1,), (1,)), ((), ()))
    head = pl.program_id(0)

    @pl.when(head == 0)
    def _():
        for r in range(4):
            place = pl.multiple_of((scalars[1] ^ r) * quarter, quarter)
            grad_mixed[:, pl.ds(place, quarter)] = pieces[r][...]

    first_row = pl.multiple_of(head * HEAD, HEAD)
    keys = qkv_ref[pl.ds(inner_rows + first_row, HEAD), :]
    key_rows[pl.ds(0, pad), :] = jnp.zeros((pad, HEAD), BF16)
    value_rows[pl.ds(0, pad), :] = jnp.zeros((pad, HEAD), BF16)
    key_pad[:, pl.ds(0, pad)] = jnp.zeros((HEAD, pad), BF16)
    key_rows[pl.ds(pad, group), :] = keys.T
    value_rows[pl.ds(pad, group), :] = qkv_ref[pl.ds(2 * inner_rows + first_row, HEAD), :].T
    key_pad[:, pl.ds(pad, group)] = keys
    grad_key[...] = jnp.zeros_like(grad_key)
    grad_value[...] = jnp.zeros_like(grad_value)

    def one(i, carry):
        first = pl.multiple_of(i * block, block)

        def body(window):
            begin = pl.multiple_of(first + pad + block - window, block)
            query = qkv_ref[pl.ds(first_row, HEAD), pl.ds(first, block)]
            grad = grad_mixed[pl.ds(first_row, HEAD), pl.ds(first, block)]
            scores = jnp.dot(key_rows[pl.ds(begin, window), :], query, preferred_element_type=F32)
            allowed = scores_mask(begin - pad, first, window, block, scalars)
            exponent = scores * 0.125 - lse_ref[0, :, pl.ds(first, block)]
            probs = jnp.exp(jnp.where(allowed, exponent, NEGATIVE))
            grad_probs = jnp.dot(
                value_rows[pl.ds(begin, window), :], grad, preferred_element_type=F32
            )
            inner = jnp.sum(probs * grad_probs, axis=0, keepdims=True)
            raw = (0.125 * (probs * (grad_probs - inner))).astype(BF16)
            grad_query = jnp.dot(
                key_pad[:, pl.ds(begin, window)], raw, preferred_element_type=F32
            )
            column = pl.multiple_of(first % quarter, block)
            piece = (first // quarter) ^ scalars[1]
            out_ref[piece, 0, :, pl.ds(column, block)] = grad_query.astype(BF16)
            grad_value[:, pl.ds(begin, window)] += lax.dot_general(
                grad, probs.astype(BF16), contract_last, preferred_element_type=F32
            )
            grad_key[:, pl.ds(begin, window)] += lax.dot_general(
                query, raw, contract_last, preferred_element_type=F32
            )

        for_window(first, block, pad, scalars, body)
        return carry

    lax.fori_loop(0, group // block, one, 0)
    for j in range(4):
        piece = scalars[1] ^ j
        out_ref[piece, 1] = grad_key[:, pl.ds(pad + j * quarter, quarter)].astype(BF16)
        out_ref[piece, 2] = grad_value[:, pl.ds(pad + j * quarter, quarter)].astype(BF16)


def attend_back(scalars, qkv, lse, pieces, heads):
    group = qkv.shape[1]
    block = 256

    def whole(shape):
        return pl.BlockSpec(
            shape, lambda i, _: (0,) * len(shape), pipeline_mode=pl.Buffered(1)
        )

    return pl.pallas_call(
        functools.partial(attend_back_kernel, block, MAXLEN),
        grid_spec=pltpu.PrefetchScalarGridSpec(
            num_scalar_prefetch=1,
            grid=(heads,),
            in_specs=[
                whole(qkv.shape),
                pl.BlockSpec((1, 1, group), lambda h, _: (h, 0, 0)),
                *[whole(item.shape) for item in pieces],
            ],
            out_specs=pl.BlockSpec((4, 3, HEAD, group // 4), lambda h, _: (0, 0, h, 0)),
            scratch_shapes=[
                pltpu.VMEM((heads * HEAD, group), BF16),
                pltpu.VMEM((MAXLEN + group, HEAD), BF16),
                pltpu.VMEM((MAXLEN + group, HEAD), BF16),
                pltpu.VMEM((HEAD, MAXLEN + group), BF16),
                pltpu.VMEM((HEAD, MAXLEN + group), F32),
                pltpu.VMEM((HEAD, MAXLEN + group), F32),
            ],
        ),
        out_shape=jax.ShapeDtypeStruct((4, 3, heads * HEAD, group // 4), BF16),
        compiler_params=pltpu.CompilerParams(vmem_limit_bytes=48 * 2**20),
        cost_estimate=cost_of(34),
        name="attend_back",
    )(scalars, qkv, lse, *pieces)


def mixed_back_kernel(scalars, grad_ref, p0, p1, p2, p3, *refs):
    outs, weight = refs[:4], refs[4]
    rows = p0.shape[2]
    for r, shards in enumerate((p0, p1, p2, p3)):
        for k in range(SHARDS):
            place = pl.multiple_of((scalars[0] ^ k) * rows, rows)
            weight[pl.ds(place, rows), :] = shards[k % LOW, k // LOW]
        outs[r][...] = lax.dot_general(
            weight[...].T, grad_ref[...], (((1,), (1,)), ((), ())), preferred_element_type=F32
        ).astype(BF16)


def mixed_back(scalars, grad, weights):
    rows, width = grad.shape
    inner = weights[0].shape[3]

    def whole(shape):
        return pl.BlockSpec(shape, lambda i, _: (0,) * len(shape))

    return pl.pallas_call(
        mixed_back_kernel,
        grid_spec=pltpu.PrefetchScalarGridSpec(
            num_scalar_prefetch=1,
            grid=(1,),
            in_specs=[whole(grad.shape), *[whole(item.shape) for item in weights]],
            out_specs=[whole((inner, rows)) for _ in range(4)],
            scratch_shapes=[pltpu.VMEM((width, inner), BF16)],
        ),
        out_shape=[jax.ShapeDtypeStruct((inner, rows), BF16) for _ in range(4)],
        compiler_params=pltpu.CompilerParams(vmem_limit_bytes=32 * 2**20),
        cost_estimate=cost_of(4),
        name="mixed_back",
    )(scalars, grad, *weights)


def inputs_back_kernel(g0, g1, g2, g3, p0, p1, p2, p3, x_ref, gain_ref, hidden_ref, out_ref, sum_ref):
    total = 0.0
    for grad, weight in zip((g0, g1, g2, g3), (p0, p1, p2, p3)):
        total += jnp.dot(grad[...].T, weight[...], preferred_element_type=F32)
    x = x_ref[...]
    scale = lax.rsqrt(jnp.mean(x * x, axis=1, keepdims=True) + EPSILON)
    through = total * gain_ref[...]
    inner = jnp.mean(through * x, axis=1, keepdims=True)
    out_ref[...] = hidden_ref[...] + scale * through - (scale * scale * scale * inner) * x
    sum_ref[0] = jnp.sum(total * x * scale, axis=0, keepdims=True)


def inputs_back(grads, weights, x, gain, grad_hidden):
    rows, width = x.shape
    block = rows // 2

    def whole(shape):
        return pl.BlockSpec(shape, lambda i: (0,) * len(shape), pipeline_mode=pl.Buffered(1))

    part = pl.BlockSpec((block, width), lambda i: (i, 0))
    return pl.pallas_call(
        inputs_back_kernel,
        grid=(2,),
        in_specs=[
            *[pl.BlockSpec((item.shape[0], block), lambda i: (0, i)) for item in grads],
            *[whole(item.shape) for item in weights],
            part,
            whole(gain.shape),
            part,
        ],
        out_specs=[part, pl.BlockSpec((1, 1, width), lambda i: (i, 0, 0))],
        out_shape=[
            jax.ShapeDtypeStruct(x.shape, F32),
            jax.ShapeDtypeStruct((2, 1, width), F32),
        ],
        compiler_params=pltpu.CompilerParams(vmem_limit_bytes=48 * 2**20),
        cost_estimate=cost_of(6),
        name="inputs_back",
    )(*grads, *weights, x, gain, grad_hidden)


def expert_kernel(
    kinds, scalars, w_gate, *refs
):
    near_pieces, far_pieces, refs = refs[:2], refs[2:6], refs[6:]
    x_blocks, g_blocks, g_core = refs[: 2 * LOW], refs[2 * LOW : 3 * LOW], refs[3 * LOW]
    refs = refs[3 * LOW + 1 :]
    back_own, back_send, feed_own, feed_send, grads_out, *refs = refs
    x_all, g_all, x_t, g_t, weights, hidden, acc_feed, acc_back, scales, plain = refs
    slots, width = feed_own.shape
    block = slots // LOW
    half = width // 2
    step = pl.program_id(0)
    contract_last = (((1,), (1,)), ((), ()))
    units = weights.shape[2]

    def weight_column(x_ref):
        extra = x_ref[:, width:].astype(F32)
        lanes = lax.broadcasted_iota(jnp.int32, extra.shape, 1)
        named = (lanes == scalars[0]) | (lanes == scalars[0] + kinds)
        return jnp.sum(jnp.where(named, extra, 0.0), axis=1, keepdims=True)

    @pl.when(step == 0)
    def _():
        for i in range(2 * LOW):
            rows = pl.ds(i * block, block)
            scale = weight_column(x_blocks[i])
            scales[rows, :] = jnp.broadcast_to(scale, (block, 128))
            if i < LOW:
                plain[rows, :] = g_blocks[i][...]
            else:
                plain[rows, :] = g_core[pl.ds((i - LOW) * block, block), :]
            x_all[rows, :] = x_blocks[i][:, :width]
            g_all[rows, :] = (plain[rows, :].astype(F32) * scale).astype(BF16)
        x_t[...] = x_all[...].T
        g_t[...] = g_all[...].T
        acc_feed[...] = jnp.zeros_like(acc_feed)
        acc_back[...] = jnp.zeros_like(acc_back)

    for i in range(2):
        rows = pl.ds(i * half, half)
        weights[0, rows, :] = w_gate[:, 0, i].reshape(half, units)
    near = pl.multiple_of(scalars[1] * half, half)
    for k in range(2):
        weights[k + 1, pl.ds(near, half), :] = near_pieces[k][:, 0].reshape(half, units)
        place = (1 - scalars[1]) * half
        for piece in far_pieces[2 * k : 2 * k + 2]:
            rows = piece.shape[0] * half // LOW
            weights[k + 1, pl.ds(pl.multiple_of(place, half // LOW), rows), :] = piece[
                :, 0
            ].reshape(rows, units)
            place += rows

    for part in range(2):
        rows = pl.ds(part * slots, slots)
        x = x_all[rows, :]
        gate = jnp.dot(x, weights[0], preferred_element_type=F32)
        up = jnp.dot(x, weights[1], preferred_element_type=F32)
        grad_act = jnp.dot(g_all[rows, :], weights[2], preferred_element_type=F32)
        sig = jax.nn.sigmoid(gate)
        silu = gate * sig
        active = (silu * up).astype(BF16)
        grad_gate = (grad_act * up * (sig * (1.0 + gate * (1.0 - sig)))).astype(BF16)
        grad_up = (grad_act * silu).astype(BF16)
        hidden[0, rows, :] = grad_gate
        hidden[1, rows, :] = grad_up
        hidden[2, rows, :] = active
        acc_feed[rows, :] += lax.dot_general(
            active, weights[2], contract_last, preferred_element_type=F32
        )
        acc_back[rows, :] += lax.dot_general(
            grad_gate, weights[0], contract_last, preferred_element_type=F32
        ) + lax.dot_general(grad_up, weights[1], contract_last, preferred_element_type=F32)

    for k in range(3):
        left = (g_t if k == 2 else x_t)
        grad = jnp.dot(left[...], hidden[k], preferred_element_type=F32).astype(BF16)
        for i in range(2):
            part = grad[i * half : (i + 1) * half].reshape(LOW, -1, units)
            grads_out[i, :, 0, k] = part

    @pl.when(step == pl.num_programs(0) - 1)
    def _():
        for part in range(2):
            rows = pl.ds(part * slots, slots)
            feed = acc_feed[rows, :]
            inner = jnp.sum(feed * plain[rows, :].astype(F32), axis=1, keepdims=True)
            feed = feed * scales[rows, 0:1]
            lanes = lax.broadcasted_iota(jnp.int32, (slots, 128), 1)
            if part == 0:
                back_own[:, :width] = acc_back[rows, :]
                back_own[:, width:] = jnp.where(lanes == scalars[0], inner, 0.0)
                feed_own[...] = feed
            else:
                high = inner.astype(BF16).astype(F32)
                extra = jnp.where(lanes == scalars[0], high, 0.0)
                extra = jnp.where(lanes == scalars[0] + kinds, inner - high, extra)
                back_send[:, :width] = acc_back[rows, :].astype(BF16)
                back_send[:, width:] = extra.astype(BF16)
                feed_send[...] = feed.astype(BF16)


def expert_pass(kinds, scalars, x_blocks, g_blocks, w_gate, w_near, w_far):
    block, width = g_blocks[0].shape
    slots = LOW * block
    low, parities, _, shard_rows, shard_units = w_gate.shape
    units = 512
    steps = shard_units // units

    def whole(shape):
        return pl.BlockSpec(
            shape, lambda i, _: (0,) * len(shape), pipeline_mode=pl.Buffered(1)
        )

    grads_spec = pl.BlockSpec(
        (2, low, 1, 3, shard_rows, units), lambda i, _: (0, 0, i // steps, 0, 0, i % steps)
    )
    gate_spec = pl.BlockSpec(
        (low, 1, 2, shard_rows, units), lambda i, _: (0, i // steps, 0, 0, i % steps)
    )
    def up_spec(count):
        return pl.BlockSpec(
            (count, 1, shard_rows, units), lambda i, _: (0, i // steps, 0, i % steps)
        )

    wide = width + 128
    return pl.pallas_call(
        functools.partial(expert_kernel, kinds),
        grid_spec=pltpu.PrefetchScalarGridSpec(
            num_scalar_prefetch=1,
            grid=(parities * steps,),
            in_specs=[
                gate_spec,
                *[up_spec(item.shape[0]) for item in (*w_near, *w_far)],
                *[whole((block, wide)) for _ in range(2 * LOW)],
                *[whole(item.shape) for item in g_blocks],
            ],
            out_specs=[
                whole((slots, wide)),
                whole((slots, wide)),
                whole((slots, width)),
                whole((slots, width)),
                grads_spec,
            ],
            scratch_shapes=[
                pltpu.VMEM((2 * slots, width), BF16),
                pltpu.VMEM((2 * slots, width), BF16),
                pltpu.VMEM((width, 2 * slots), BF16),
                pltpu.VMEM((width, 2 * slots), BF16),
                pltpu.VMEM((3, width, units), BF16),
                pltpu.VMEM((3, 2 * slots, units), BF16),
                pltpu.VMEM((2 * slots, width), F32),
                pltpu.VMEM((2 * slots, width), F32),
                pltpu.VMEM((2 * slots, 128), F32),
                pltpu.VMEM((2 * slots, width), BF16),
            ],
        ),
        out_shape=[
            jax.ShapeDtypeStruct((slots, wide), F32),
            jax.ShapeDtypeStruct((slots, wide), BF16),
            jax.ShapeDtypeStruct((slots, width), F32),
            jax.ShapeDtypeStruct((slots, width), BF16),
            jax.ShapeDtypeStruct((2, low, parities, 3, shard_rows, shard_units), BF16),
        ],
        compiler_params=pltpu.CompilerParams(vmem_limit_bytes=58 * 2**20),
        cost_estimate=cost_of(35),
        name="expert_pass",
    )(scalars, w_gate, *w_near, *w_far, *x_blocks, *g_blocks)


def pick_kernel(ids_ref, *refs):
    pieces, outs = refs[:4], refs[4:]
    block = outs[0].shape[0]
    rows = pieces[0].shape[0]
    for i, out_ref in enumerate(outs):
        slot = i * block + lax.broadcasted_iota(jnp.int32, (block, rows), 0)
        total = 0.0
        for r in range(4):
            columns = pl.ds(r * rows, rows)
            held = (slot == ids_ref[0:1, columns]) | (slot == ids_ref[1:2, columns])
            held = jnp.where(held, 1.0, 0.0).astype(BF16)
            total += jnp.dot(held, pieces[r][...], preferred_element_type=F32)
        out_ref[...] = total.astype(BF16)


def pick(ids, pieces, slots):
    rows, width = pieces[0].shape
    block = slots // LOW

    def whole(shape):
        return pl.BlockSpec(shape, lambda i: (0, 0))

    return pl.pallas_call(
        pick_kernel,
        grid=(1,),
        in_specs=[whole((8, 4 * rows)), *[whole((rows, width)) for _ in range(4)]],
        out_specs=[whole((block, width)) for _ in range(LOW)],
        out_shape=[jax.ShapeDtypeStruct((block, width), BF16) for _ in range(LOW)],
        compiler_params=pltpu.CompilerParams(vmem_limit_bytes=32 * 2**20),
        cost_estimate=cost_of(5),
        name="pick",
    )(ids, *pieces)


def to_experts(blocks):
    return [blocks[0]] + [flip(blocks[b], "lo", LOW, b) for b in range(1, LOW)]


def to_heads(blocks):
    return [blocks[0]] + [
        lax.ppermute(blocks[r], ("y", "c"), [(i, i ^ r) for i in range(4)]) for r in range(1, 4)
    ]


def back_sum_kernel(kinds, own_ref, core_ref, *outs):
    width = own_ref.shape[1] - 128
    block = outs[0].shape[0]
    for i, out_ref in enumerate(outs):
        rows = pl.ds(i * block, block)
        out_ref[:, :width] = (
            own_ref[rows, :width] + core_ref[rows, :width].astype(F32)
        ).astype(BF16)
        extra = own_ref[rows, width:] + core_ref[rows, width:].astype(F32)
        lanes = lax.broadcasted_iota(jnp.int32, extra.shape, 1)
        high = jnp.where(lanes < kinds, extra, 0.0).astype(BF16).astype(F32)
        low = jnp.where(lanes < kinds, extra - high, 0.0)
        low = pltpu.roll(low, kinds, 1) + jnp.where(lanes >= kinds, extra, 0.0)
        out_ref[:, width:] = (high + low).astype(BF16)


def back_sum(kinds, own, core):
    slots, wide = own.shape
    block = slots // LOW

    def whole(shape):
        return pl.BlockSpec(shape, lambda i: (0, 0))

    return pl.pallas_call(
        functools.partial(back_sum_kernel, kinds),
        grid=(1,),
        in_specs=[whole(own.shape), whole(core.shape)],
        out_specs=[whole((block, wide)) for _ in range(LOW)],
        out_shape=[jax.ShapeDtypeStruct((block, wide), BF16) for _ in range(LOW)],
        compiler_params=pltpu.CompilerParams(vmem_limit_bytes=32 * 2**20),
        cost_estimate=cost_of(3),
        name="back_sum",
    )(own, core)


def feed_sum_kernel(own_ref, core_ref, *outs):
    block = outs[0].shape[0]
    for i, out_ref in enumerate(outs):
        rows = pl.ds(i * block, block)
        out_ref[...] = (own_ref[rows, :] + core_ref[rows, :].astype(F32)).astype(BF16)


def feed_sum(own, core):
    slots, width = own.shape
    block = slots // LOW

    def whole(shape):
        return pl.BlockSpec(shape, lambda i: (0, 0))

    return pl.pallas_call(
        feed_sum_kernel,
        grid=(1,),
        in_specs=[whole(own.shape), whole(core.shape)],
        out_specs=[whole((block, width)) for _ in range(LOW)],
        out_shape=[jax.ShapeDtypeStruct((block, width), BF16) for _ in range(LOW)],
        compiler_params=pltpu.CompilerParams(vmem_limit_bytes=32 * 2**20),
        cost_estimate=cost_of(3),
        name="feed_sum",
    )(own, core)


def spread_kernel(ids_ref, *refs):
    blocks, (near_ref, send_ref, slots_ref) = refs[:LOW], refs[LOW:]
    rows = near_ref.shape[1]
    slots = slots_ref.shape[0]
    block = slots // LOW

    @pl.when(pl.program_id(0) == 0)
    def _():
        for i in range(LOW):
            slots_ref[pl.ds(i * block, block), :] = blocks[i][...]

    for k, out_ref in enumerate((near_ref, send_ref)):
        slot = lax.broadcasted_iota(jnp.int32, (rows, slots), 1)
        ids = ids_ref[pl.ds(k * rows, rows), :]
        held = (slot == ids[:, 0:1]) | (slot == ids[:, 1:2])
        held = jnp.where(held, 1.0, 0.0).astype(BF16)
        total = jnp.dot(held, slots_ref[...], preferred_element_type=F32)
        out_ref[0] = total.astype(out_ref.dtype)


def spread(ids, values, rows):
    block, width = values[0].shape
    return pl.pallas_call(
        spread_kernel,
        grid=(2,),
        in_specs=[
            pl.BlockSpec((2 * rows, 8), lambda i: (i, 0)),
            *[pl.BlockSpec((block, width), lambda i: (0, 0)) for _ in range(LOW)],
        ],
        out_specs=[
            pl.BlockSpec((1, rows, width), lambda i: (i, 0, 0)),
            pl.BlockSpec((1, rows, width), lambda i: (i, 0, 0)),
        ],
        out_shape=[
            jax.ShapeDtypeStruct((2, rows, width), F32),
            jax.ShapeDtypeStruct((2, rows, width), BF16),
        ],
        scratch_shapes=[pltpu.VMEM((LOW * block, width), BF16)],
        compiler_params=pltpu.CompilerParams(vmem_limit_bytes=32 * 2**20),
        cost_estimate=cost_of(30),
        name="spread",
    )(ids, *values)


def slots_kernel(experts, capacity, scalars, routes_col, order_col, routes_row, order_row,
                 row_ref, col_ref, places_ref):
    group = routes_row.shape[1]
    rows = group // 4
    share = capacity // 2
    span = 2 * group
    bound = scalars[BOUNDS + 2]

    def target_of(routes, axis):
        place = lax.broadcasted_iota(jnp.int32, routes.shape, axis)
        return jnp.where((routes < experts) & (place < bound), routes, experts)

    target = target_of(routes_row[...], 1)
    code = target * span + order_row[...]
    block = 256

    def count(i, carry):
        first = pl.multiple_of(i * block, block)
        routes = routes_col[pl.ds(first, block), :]
        place = first + lax.broadcasted_iota(jnp.int32, routes.shape, 0)
        held = jnp.where((routes < experts) & (place < bound), routes, experts)
        others = held * span + order_col[pl.ds(first, block), :]
        result = []
        for k in range(2):
            total = carry[k]
            for j in range(2):
                smaller = jnp.where(others[:, j : j + 1] < code[k : k + 1, :], 1.0, 0.0)
                total = total + jnp.sum(smaller, axis=0, keepdims=True)
            result.append(total)
        return tuple(result)

    zero = jnp.zeros((1, group), F32)
    counts = lax.fori_loop(0, group // block, count, (zero, zero))
    for k in range(2):
        mine_target = target[k : k + 1, :]
        base = jnp.zeros((1, group), F32)
        for e in range(1, experts):
            earlier = jnp.sum(jnp.where(target < e, 1.0, 0.0))
            base = jnp.where(mine_target == e, earlier, base)
        place = (counts[k] - base).astype(jnp.int32)
        first = scalars[3] * share
        held = (
            (mine_target < experts)
            & (place >= first)
            & (place < first + share)
            & (place < capacity)
            & (jnp.bitwise_and(mine_target, 1) == scalars[2])
        )
        block = jnp.bitwise_xor(lax.shift_right_logical(mine_target, 1), scalars[LOW_PLACE])
        slot = block * share + place - first
        places_ref[k : k + 1, :] = jnp.where(held, slot, -1)
    for r in range(4):
        start = pl.multiple_of((scalars[1] ^ r) * rows, rows)
        piece = places_ref[:, pl.ds(start, rows)]
        row_ref[:, pl.ds(r * rows, rows)] = piece
        col_ref[pl.ds(r * rows, rows), :] = piece.T


def slots_of(scalars, routes, drop_order, experts, capacity):
    group = routes.shape[0]
    whole = pl.BlockSpec(memory_space=pltpu.VMEM)
    return pl.pallas_call(
        functools.partial(slots_kernel, experts, capacity),
        in_specs=[pl.BlockSpec(memory_space=pltpu.SMEM)] + [whole] * 4,
        out_specs=[whole] * 2,
        out_shape=[
            jax.ShapeDtypeStruct((8, group), jnp.int32),
            jax.ShapeDtypeStruct((group, 8), jnp.int32),
        ],
        scratch_shapes=[pltpu.VMEM((8, group), jnp.int32)],
        compiler_params=pltpu.CompilerParams(vmem_limit_bytes=32 * 2**20),
        cost_estimate=cost_of(8),
        name="slots",
    )(scalars, routes, drop_order, routes.T, drop_order.T)


def middle_kernel(kinds, scalars, mixed, p0, p1, p2, p3, x_ref, gain_ref, router_w, prior_ref,
                  prior_w, hidden_ref, sent_ref, router_ref, weight):
    hidden = x_ref[...]
    rows = p0.shape[2]
    for r, shards in enumerate((p0, p1, p2, p3)):
        for k in range(SHARDS):
            place = pl.multiple_of((scalars[0] ^ k) * rows, rows)
            weight[r, pl.ds(place, rows), :] = shards[k % LOW, k // LOW]
        hidden += lax.dot_general(
            mixed[scalars[1] ^ r].T, weight[r], (((1,), (1,)), ((), ())),
            preferred_element_type=F32,
        )
    hidden_ref[...] = hidden
    scale = lax.rsqrt(jnp.mean(hidden * hidden, axis=1, keepdims=True) + EPSILON)
    rounded = (hidden * scale * gain_ref[...]).astype(BF16)
    width = hidden.shape[1]
    sent_ref[:, :width] = rounded
    router_high, router_low = halves(router_w[...])
    logits = (
        jnp.dot(rounded, router_high, preferred_element_type=F32)
        + jnp.dot(rounded, router_low, preferred_element_type=F32)
        + split_dot(prior_ref[...], prior_w[...])
    )
    lanes = lax.broadcasted_iota(jnp.int32, logits.shape, 1)
    logits = jnp.where(lanes < 2 * kinds, logits, NEGATIVE)
    weights = jnp.exp(logits - jnp.max(logits, axis=1, keepdims=True))
    total = jnp.sum(jnp.where(lanes < kinds, weights, 0.0), axis=1, keepdims=True)
    router = weights / total
    router_ref[...] = router
    high = router.astype(BF16).astype(F32)
    sent_ref[:, width:] = jnp.where(lanes < kinds, high, router - high).astype(BF16)


def middle(kinds, scalars, mixed, weights, x, gain, router_w, prior, prior_w):
    rows, width = x.shape
    lanes = router_w.shape[1]

    def whole(shape):
        return pl.BlockSpec(shape, lambda i, _: (0,) * len(shape))

    return pl.pallas_call(
        functools.partial(middle_kernel, kinds),
        grid_spec=pltpu.PrefetchScalarGridSpec(
            num_scalar_prefetch=1,
            grid=(1,),
            in_specs=[
                whole(mixed.shape),
                *[whole(item.shape) for item in weights],
                whole(x.shape),
                whole(gain.shape),
                whole(router_w.shape),
                pl.BlockSpec((rows, kinds), lambda i, scalars: (scalars[1], 0)),
                whole(prior_w.shape),
            ],
            out_specs=[whole((rows, width)), whole((rows, width + lanes)), whole((rows, lanes))],
            scratch_shapes=[pltpu.VMEM((4, width, mixed.shape[1]), BF16)],
        ),
        out_shape=[
            jax.ShapeDtypeStruct((rows, width), F32),
            jax.ShapeDtypeStruct((rows, width + lanes), BF16),
            jax.ShapeDtypeStruct((rows, lanes), F32),
        ],
        compiler_params=pltpu.CompilerParams(vmem_limit_bytes=48 * 2**20),
        cost_estimate=cost_of(6),
        name="middle",
    )(scalars, mixed, *weights, x, gain, router_w, prior, prior_w)


def halves(value):
    high = value.astype(BF16)
    return high, (value - high.astype(F32)).astype(BF16)


def split_dot(left, right):
    (left_high, left_low), (right_high, right_low) = halves(left), halves(right)
    return (
        jnp.dot(left_high, right_high, preferred_element_type=F32)
        + jnp.dot(left_low, right_high, preferred_element_type=F32)
        + jnp.dot(left_high, right_low, preferred_element_type=F32)
    )


def turned_dot(left, right):
    high, low = halves(left.T)
    return jnp.dot(high, right, preferred_element_type=F32) + jnp.dot(
        low, right, preferred_element_type=F32
    )


def router_back_kernel(kinds, experts, scalars, near_ref, got_ref, far_ref, hidden_ref, router_ref,
                       routes_ref, cotangent_ref, prior_ref, gain_ref, small_ref, small_t_ref,
                       vector_ref, prior_w_ref,
                       grad_hidden_ref, grad_low_ref, partial_ref, grad_prior_ref, sums_ref):
    step = pl.program_id(0)
    rows, width = hidden_ref.shape
    place = scalars[1] * rows * pl.num_programs(0) + step * rows
    valid = place + lax.broadcasted_iota(jnp.int32, (rows, 1), 0) < scalars[BOUNDS + 2]
    valid = jnp.where(valid, 1.0, 0.0)
    back = near_ref[0] + got_ref[0].astype(F32) + far_ref[...].astype(F32)
    hidden = hidden_ref[...]
    grad_out = cotangent_ref[...] * valid
    scale = lax.rsqrt(jnp.mean(hidden * hidden, axis=1, keepdims=True) + EPSILON)
    unit = hidden * scale
    normed = unit * gain_ref[...]
    router = router_ref[...]
    lanes = lax.broadcasted_iota(jnp.int32, router.shape, 1)
    routes = routes_ref[...]

    def column(array, k):
        return jnp.sum(jnp.where(lanes == k, array, 0.0), axis=1, keepdims=True)

    def named(kind):
        return jnp.where((routes[:, 0:1] == kind) | (routes[:, 1:2] == kind), 1.0, 0.0)

    copy, first, second = (named(experts + k) for k in (1, 2, 3))
    weight_copy = column(router, experts + 1) * copy
    weight_first = column(router, experts + 2) * first
    weight_second = column(router, experts + 3) * second
    mixlog = split_dot(normed, small_ref[...])

    def softmax_two(k):
        one, two = column(mixlog, k), column(mixlog, k + 1)
        highest = jnp.maximum(one, two)
        one, two = jnp.exp(one - highest), jnp.exp(two - highest)
        return one / (one + two), two / (one + two)

    mix_one, mix_two = softmax_two(kinds), softmax_two(kinds + 2)
    vector_one, vector_two = vector_ref[0:1, :], vector_ref[1:2, :]
    along = jnp.sum(normed * grad_out, axis=1, keepdims=True)
    along_one = jnp.sum(vector_one * grad_out, axis=1, keepdims=True)
    along_two = jnp.sum(vector_two * grad_out, axis=1, keepdims=True)

    extra = back[:, width:]
    pairs = jnp.where(lanes < kinds, extra, 0.0) + jnp.where(
        lanes < kinds, pltpu.roll(extra, extra.shape[1] - kinds, 1), 0.0
    )
    grad_router = pairs + jnp.where(lanes == experts + 1, copy * along, 0.0)
    grad_router += jnp.where(
        lanes == experts + 2, first * (mix_one[0] * along + mix_one[1] * along_one), 0.0
    )
    grad_router += jnp.where(
        lanes == experts + 3, second * (mix_two[0] * along + mix_two[1] * along_two), 0.0
    )
    held = jnp.where(lanes < kinds, router, 0.0)
    grad_small = held * (grad_router - jnp.sum(held * grad_router, axis=1, keepdims=True))
    grad_prior_ref[...] = split_dot(grad_small, prior_w_ref[...])[:, :kinds]
    grad_logits = grad_small

    def mixed_back(weight, mix, other, k):
        one, two = weight * along, weight * other
        inner = mix[0] * one + mix[1] * two
        return jnp.where(lanes == k, mix[0] * (one - inner), 0.0) + jnp.where(
            lanes == k + 1, mix[1] * (two - inner), 0.0
        )

    grad_mixlog = mixed_back(weight_first, mix_one, along_one, kinds) + mixed_back(
        weight_second, mix_two, along_two, kinds + 2
    )
    grad_small = grad_logits + grad_mixlog
    share = weight_copy + weight_first * mix_one[0] + weight_second * mix_two[0]
    grad_normed = (
        back[:, :width]
        + share * grad_out
        + split_dot(grad_small, small_t_ref[...])
    )
    through = grad_normed * gain_ref[...]
    inner = jnp.mean(through * hidden, axis=1, keepdims=True)
    grad_hidden = grad_out + scale * through - (scale * scale * scale * inner) * hidden
    grad_hidden_ref[...] = grad_hidden
    grad_low_ref[...] = grad_hidden.astype(BF16)
    vector_first, vector_second = weight_first * mix_one[1], weight_second * mix_two[1]
    partial_ref[...] = valid * (
        hidden + share * normed + vector_first * vector_one + vector_second * vector_two
    )

    @pl.when(step == 0)
    def _():
        sums_ref[...] = jnp.zeros_like(sums_ref)

    vectors = jnp.where(lanes == kinds + 5, vector_first, 0.0) + jnp.where(
        lanes == kinds + 6, vector_second, 0.0
    )
    low = normed.astype(BF16)
    total = turned_dot(grad_small, low) + turned_dot(vectors, grad_out.astype(BF16))
    sums_ref[: kinds + 8, :] += total[: kinds + 8, :]
    sums_ref[kinds + 4 : kinds + 5, :] += jnp.sum(grad_normed * unit, axis=0, keepdims=True)
    prior = split_dot(prior_ref[...].T, grad_logits)
    sums_ref[pl.ds(kinds + 8, kinds), : lanes.shape[1]] += prior


def router_back(kinds, experts, scalars, near, got, far, hidden, router, routes, cotangent, prior,
                gain, small, small_t, vector, prior_w):
    rows, width = hidden.shape
    block = rows // 2
    lanes = router.shape[1]

    def whole(shape):
        return pl.BlockSpec(shape, lambda i, _: (0,) * len(shape))

    def part(columns):
        return pl.BlockSpec((block, columns), lambda i, _: (i, 0))

    def mine(columns):
        return pl.BlockSpec((block, columns), lambda i, scalars: (scalars[1] * 2 + i, 0))

    return pl.pallas_call(
        functools.partial(router_back_kernel, kinds, experts),
        grid_spec=pltpu.PrefetchScalarGridSpec(
            num_scalar_prefetch=1,
            grid=(2,),
            in_specs=[
                pl.BlockSpec((1, block, width + lanes), lambda i, _: (0, i, 0)),
                pl.BlockSpec((1, block, width + lanes), lambda i, _: (0, i, 0)),
                part(width + lanes),
                part(width),
                part(lanes),
                mine(2),
                part(width),
                mine(kinds),
                whole(gain.shape),
                whole(small.shape),
                whole(small_t.shape),
                whole(vector.shape),
                whole(prior_w.shape),
            ],
            out_specs=[
                part(width),
                part(width),
                part(width),
                part(kinds),
                whole((32, width)),
            ],
        ),
        out_shape=[
            jax.ShapeDtypeStruct((rows, width), F32),
            jax.ShapeDtypeStruct((rows, width), BF16),
            jax.ShapeDtypeStruct((rows, width), F32),
            jax.ShapeDtypeStruct((rows, kinds), F32),
            jax.ShapeDtypeStruct((32, width), F32),
        ],
        compiler_params=pltpu.CompilerParams(vmem_limit_bytes=48 * 2**20),
        cost_estimate=cost_of(8),
        name="router_back",
    )(scalars, near, got, far, hidden, router, routes, cotangent, prior, gain, small, small_t,
      vector, prior_w)


def two_parts(value):
    high = lax.reduce_precision(value, 8, 7)
    return jnp.concatenate([high, value - high], axis=-1).astype(BF16)


def everywhere(value, axes, count):
    copies = jnp.broadcast_to(value[None], (count, *value.shape))
    return lax.all_to_all(copies, axes, 0, 0, tiled=True)


def flip(value, axis, size, bit):
    return lax.ppermute(value, axis, [(i, i ^ bit) for i in range(size)])


def by_halves(value):
    if value.shape[0] == 2:
        return value
    rows, units = value.shape[-2:]
    middle_axes = tuple(range(2, value.ndim - 2))
    turned = value.transpose(*middle_axes, 0, 1, value.ndim - 2, value.ndim - 1)
    turned = turned.reshape(*turned.shape[:-4], 2, LOW, value.shape[0] * rows // 2, units)
    axes = turned.ndim
    return turned.transpose(axes - 4, axes - 3, *range(axes - 4), axes - 2, axes - 1)


def scatter_high(value, many):
    if many != 2:
        rows, units = value.shape[-2:]
        middle_axes = tuple(range(2, value.ndim - 2))
        turned = value.transpose(*middle_axes, 0, 1, value.ndim - 2, value.ndim - 1)
        turned = turned.reshape(*turned.shape[:-4], many, LOW, 2 * rows // many, units)
        axes = turned.ndim
        value = turned.transpose(axes - 4, axes - 3, *range(axes - 4), axes - 2, axes - 1)
    return lax.psum_scatter(value, "hi", scatter_dimension=0)


def gather_rows(value, later, many):
    if many != 2:
        full = lax.all_gather(value, ("hi", "lo"), axis=0, tiled=True)
        full = full.reshape(2, LOW, -1, full.shape[1])
        return [full[:, i] for i in range(LOW)], later
    far, *later = lax.optimization_barrier((swap(value, "hi"), *later))
    both = jnp.stack([value, far])
    return [both] + [flip(both, "lo", LOW, bit) for bit in range(1, LOW)], tuple(later)


def scatter_rows(near, far, many):
    if many != 2:
        full = jnp.stack([near, far]).astype(F32).reshape(-1, near.shape[2])
        return lax.psum_scatter(full, ("hi", "lo"), scatter_dimension=0, tiled=True)
    both = near.astype(F32) + far.astype(F32)
    total = both[0]
    for bit in range(1, LOW):
        total = total + flip(both[bit].astype(BF16), "lo", LOW, bit).astype(F32)
    return total


def per_device(
    many,
    inputs,
    cotangent,
    lengths,
    routes,
    drop_order,
    prior_logits,
    attn_gain,
    w_query,
    w_key,
    w_value,
    w_out,
    moe_gain,
    w_router,
    w_prior,
    w_const,
    const_vector,
    w_gate,
    w_up,
    w_down,
):
    tok_rows, width = inputs.shape
    group = tok_rows * 4
    kinds = w_router.shape[1]
    experts, shard_rows, shard_units = w_gate.shape
    capacity = 3 * group // 16
    share = capacity // 2
    slots = LOW * share
    local_width = w_query.shape[1]
    heads = local_width // HEAD
    tp_axes = ("y", "c")
    all_axes = ("hi", "lo", "y", "c")
    count = many * LOW * 4
    wide = width + 128
    high = lax.axis_index("hi")
    parity = lax.axis_index("y")
    core = lax.axis_index("c")
    place_in_group = parity * 2 + core
    mine = high * LOW + lax.axis_index("lo") if many == 2 else jnp.zeros_like(high)
    boundary = jnp.cumsum(lengths[0])
    scalars = jnp.concatenate(
        [jnp.stack([mine, place_in_group, parity, core, lax.axis_index("lo")]), boundary[:-1]]
    ).astype(jnp.int32)
    gain_one, gain_two = attn_gain.reshape(1, width), moe_gain.reshape(1, width)

    valid_mine = place_in_group * tok_rows + jnp.arange(tok_rows)[:, None] < boundary[-2]
    valid_mine = valid_mine.astype(F32)

    normed_one = rms_norm(inputs, attn_gain).astype(BF16)
    normed_other = swap(normed_one, "y")
    attn_shard = jnp.concatenate([w_query, w_key, w_value, w_out.T], axis=1)
    up_part = lax.all_to_all(w_up, ("lo", "y"), 0, 0, tiled=True)
    up_part = up_part.reshape(LOW, 2, shard_rows, shard_units)
    down_shard = w_down.transpose(0, 2, 1)
    attn_shards, (w_gate,) = gather_rows(attn_shard, (w_gate,), many)
    gate_far = swap(w_gate, "hi") if many == 2 else w_gate
    router_lanes = jnp.pad(
        jnp.concatenate([w_router, w_router], axis=1), ((0, 0), (0, 128 - 2 * kinds))
    )
    prior_lanes = jnp.pad(
        jnp.concatenate([w_prior, w_prior], axis=1), ((0, 0), (0, 128 - 2 * kinds))
    )
    const_flat = w_const.transpose(1, 0, 2).reshape(width, 4)
    small = jnp.pad(
        jnp.concatenate([w_router, const_flat], axis=1), ((0, 0), (0, 128 - kinds - 4))
    )
    small_t = small.T
    prior_back = jnp.pad(w_prior.T, ((0, 128 - kinds), (0, 128 - kinds)))
    (
        attn_shards[0], scalars, router_lanes, prior_lanes, small, small_t, prior_back, prior_logits
    ) = lax.optimization_barrier(
        (attn_shards[0], scalars, router_lanes, prior_lanes, small, small_t, prior_back, prior_logits)
    )
    ids_rows, ids_cols = slots_of(scalars, routes, drop_order, experts, capacity)
    grad_out_low = (cotangent * valid_mine).astype(BF16)
    (
        normed_other, attn_shards, ids_rows, down_shard, grad_out_low, up_part, gate_far
    ) = lax.optimization_barrier(
        (normed_other, attn_shards, ids_rows, down_shard, grad_out_low, up_part, gate_far)
    )
    grad_out_other = swap(grad_out_low, "y")
    down_part = lax.all_to_all(down_shard, ("lo", "y"), 0, 0, tiled=True)
    down_part = down_part.reshape(LOW, 2, shard_rows, shard_units)
    if many == 2:
        up_far = [swap(up_part[:2], "hi"), swap(up_part[2:], "hi")]
    else:
        up_all = by_halves(lax.all_gather(up_part, "hi"))
        up_part, up_far = up_all[0], [up_all[1, :2], up_all[1, 2:]]
    out_mine = jnp.stack([item[:, :, 3 * local_width :] for item in attn_shards])
    out_other = swap(out_mine, "y")
    normed_pieces = [normed_one, swap(normed_one, "c"), normed_other, swap(normed_other, "c")]
    mixed, lse, qkv, qkv_full = attend(normed_pieces, attn_shards, scalars, heads)
    mixed, out_other, out_mine, up_far[0], down_part, grad_out_other = lax.optimization_barrier(
        (mixed, out_other, out_mine, up_far[0], down_part, grad_out_other)
    )
    if many == 2:
        high_place = high
        down_far = [swap(down_part[:2], "hi"), swap(down_part[2:], "hi")]
        gate_both = jnp.where(
            high == 0, jnp.stack([w_gate, gate_far], axis=1), jnp.stack([gate_far, w_gate], axis=1)
        )
    else:
        high_place = jnp.zeros_like(high)
        down_all = by_halves(lax.all_gather(down_part, "hi"))
        down_part, down_far = down_all[0], [down_all[1, :2], down_all[1, 2:]]
        gate_both = lax.all_gather(w_gate, "hi", axis=1)
    out_pieces = [out_mine, swap(out_mine, "c"), out_other, swap(out_other, "c")]

    mixed_mine = lax.all_to_all(mixed, tp_axes, 0, 0, tiled=True)
    grad_out_pieces = [
        grad_out_low, swap(grad_out_low, "c"), grad_out_other, swap(grad_out_other, "c"),
    ]
    grad_out_slots = pick(ids_rows, grad_out_pieces, slots)
    mixed_mine, grad_out_slots, up_far[1], gate_both = lax.optimization_barrier(
        (mixed_mine, grad_out_slots, up_far[1], gate_both)
    )

    hidden, sent_two, router = middle(
        kinds, scalars, mixed_mine, out_pieces, inputs, gain_two, router_lanes, prior_logits, prior_lanes
    )

    gate_part = lax.all_to_all(gate_both, ("lo", "y"), 0, 0, tiled=True)
    gate_part = gate_part.reshape(LOW, 2, many, shard_rows, shard_units)
    if many != 2:
        gate_part = by_halves(gate_part.transpose(2, 0, 1, 3, 4)).transpose(1, 2, 0, 3, 4)
    other_two, grad_taken, gate_part, down_far[0] = lax.optimization_barrier(
        (swap(sent_two, "y"), to_experts(grad_out_slots), gate_part, down_far[0])
    )
    pieces_two = [sent_two, swap(sent_two, "c"), other_two, swap(other_two, "c")]

    grad_taken = [*grad_taken, swap(jnp.concatenate(grad_taken), "c")]
    sent_slots = pick(ids_rows, pieces_two, slots)
    sent_slots, qkv_full = lax.optimization_barrier((sent_slots, qkv_full))
    taken = to_experts(sent_slots)
    taken += [swap(item, "c") for item in taken]
    qkv_pieces = gather_pieces(qkv_full)
    taken, qkv_pieces, down_far[1] = lax.optimization_barrier((taken, qkv_pieces, down_far[1]))

    expert = lax.axis_index("lo") * 2 + parity
    back_own, back_send, feed_own, feed_send, grads_out = expert_pass(
        kinds, jnp.stack([expert, high_place]).astype(jnp.int32), taken, grad_taken,
        gate_part, [up_part, down_part], up_far + down_far,
    )

    weight_sum = scatter_high(grads_out, many)
    back_taken = to_experts(back_sum(kinds, back_own, swap(back_send, "c")))
    feed_core = swap(feed_send, "c")
    back_taken, feed_core = lax.optimization_barrier((back_taken, feed_core))

    back_near, back_sent = spread(ids_cols, back_taken, tok_rows)
    back_got, back_other = add_core(back_near, back_sent)
    back_other, feed_core = lax.optimization_barrier((back_other, feed_core))
    back_far, feed_blocks = lax.optimization_barrier(
        (swap(back_other, "y"), feed_sum(feed_own, feed_core))
    )

    grad_hidden, grad_low, partial, grad_prior, sums = router_back(
        kinds, experts, scalars, back_near, back_got, back_far, hidden, router, routes, cotangent,
        prior_logits, gain_two, small, small_t, const_vector, prior_back,
    )
    feed_taken = to_experts(feed_blocks)
    grad_mixed = to_heads(mixed_back(scalars, grad_low, out_pieces))
    grad_mixed, grad_low = lax.optimization_barrier((grad_mixed, grad_low))
    low_other = swap(grad_low, "y")
    share_sums = lax.all_to_all(sums.reshape(count, 32 * width // count), all_axes, 0, 0, tiled=True)
    grad_qkv = attend_back(scalars, qkv, lse, grad_mixed, heads).reshape(
        4, 3 * local_width, tok_rows
    )
    grad_qkv, feed_taken, weight_sum, low_other = lax.optimization_barrier(
        (grad_qkv, feed_taken, weight_sum, low_other)
    )
    grad_attn_pieces = [grad_low, swap(grad_low, "c"), low_other, swap(low_other, "c")]

    weight_own = lax.all_to_all(
        weight_sum.reshape(2 * LOW, 3, shard_rows, shard_units), ("lo", "y"), 0, 0, tiled=True
    )
    grad_qkv_mine = to_heads(grad_qkv)
    attn_near, attn_far = attn_grads(grad_qkv, mixed, normed_pieces, grad_attn_pieces, scalars)
    if many == 2:
        attn_far = swap(attn_far, "hi")
    feed_near, feed_sent = spread(ids_cols, feed_taken, tok_rows)
    feed_got, feed_other = add_core(feed_near, feed_sent)
    (
        grad_qkv_mine, share_sums, attn_near, attn_far, feed_near, feed_got, feed_other
    ) = lax.optimization_barrier(
        (grad_qkv_mine, share_sums, attn_near, attn_far, feed_near, feed_got, feed_other)
    )
    feed_far = swap(feed_other, "y")
    share_sums = jnp.sum(share_sums, axis=0)
    grad_inputs, gain_part = inputs_back(
        grad_qkv_mine, qkv_pieces, inputs, gain_one, grad_hidden
    )
    output = partial + valid_mine * (
        feed_near[0] + feed_got[0].astype(F32) + feed_far.astype(F32)
    )
    grad_attn_own = scatter_rows(attn_near, attn_far, many)
    last = jnp.concatenate([jnp.sum(gain_part, axis=0).reshape(-1), share_sums])
    last, weight_own = lax.optimization_barrier((last, weight_own))
    last = everywhere(last, all_axes, count)
    last, grad_attn_own = lax.optimization_barrier((last, grad_attn_own))
    grad_gain = jnp.sum(last[:, :width], axis=0)
    total = last[:, width:].reshape(32, width)
    return (
        output,
        grad_inputs,
        grad_prior,
        grad_gain,
        grad_attn_own[:, :local_width],
        grad_attn_own[:, local_width : 2 * local_width],
        grad_attn_own[:, 2 * local_width : 3 * local_width],
        grad_attn_own[:, 3 * local_width :].T,
        total[kinds + 4],
        total[:kinds].T,
        total[kinds + 8 : 2 * kinds + 8, :kinds],
        total[kinds : kinds + 4].reshape(2, 2, width).transpose(0, 2, 1),
        total[kinds + 5 : kinds + 7],
        weight_own[:, 0].astype(F32),
        weight_own[:, 1].astype(F32),
        weight_own[:, 2].transpose(0, 2, 1).astype(F32),
    )


def solution(mesh):
    many = mesh.shape["fsdp"] // LOW
    fine = Mesh(mesh.devices.reshape(many, LOW, 2, 2), ("hi", "lo", "y", "c"))
    fsdp, tp = ("hi", "lo"), ("y", "c")
    every = fsdp + tp
    return jax.shard_map(
        functools.partial(per_device, many),
        mesh=fine,
        in_specs=(
            P(every, None),
            P(every, None),
            P(fsdp, None),
            P(fsdp, None),
            P(fsdp, None),
            P(fsdp, None),
            P(),
            P(fsdp, tp),
            P(fsdp, tp),
            P(fsdp, tp),
            P(tp, fsdp),
            P(),
            P(),
            P(),
            P(),
            P(),
            P(None, fsdp, tp),
            P(None, fsdp, tp),
            P(None, tp, fsdp),
        ),
        out_specs=(
            P(every, None),
            P(every, None),
            P(every, None),
            P(),
            P(fsdp, tp),
            P(fsdp, tp),
            P(fsdp, tp),
            P(tp, fsdp),
            P(),
            P(),
            P(),
            P(),
            P(),
            P(None, fsdp, tp),
            P(None, fsdp, tp),
            P(None, tp, fsdp),
        ),
        check_vma=False,
    )
```

profile of v0, /device:TPU:1, one launch (start us, length us, event | category | flops | bytes accessed | tf_op | source)
XLA Modules:
  0.0 481.9 jit_solution(3356356446028757921)
XLA Ops:
  9.8 3.1 collective-permute-start
  16.1 4.2 all-to-all-start
  31.0 10.0 %slots.1 = (s32[8,2048]{1,0:T(8,128)S(1)}, s32[2048,8]{1,0:T(8,128)S(1)}) custom-call(s32[8]{0:T(128)S(1)} %concatenate.22.scalars, s32[2048,2]{1,0:T(8,128)S(1)} %copy.52.routes_col.routes_ref, s32[2048,2]{1,0:T(8,128)S(1)} %copy.53.order_col, s32[2,2048]{1,0:T(2,128)S(1)} %bitcast.98, s32[2,2048]{1,0:T(2,128)S(1)} %bitcast.99), custom_call_target="tpu_custom_call" | custom-call | flops 9200000000 | bytes 65536 | tf_op jit(solution)/shard_map/slots/pallas_call | solution.py:776
  42.0 2.4 collective-permute-start.1
  45.5 7.3 %collective-permute-done.5.refs_7_ = bf16[2,96,768]{2,1,0:T(8,128)(2,1)} collective-permute-done((bf16[2,96,768]{2,1,0:T(8,128)(2,1)S(1)}, bf16[2,96,768]{2,1,0:T(8,128)(2,1)}, u32[]{:S(2)}, u32[]{:S(2)}) %collective-permute-start.5) | collective-permute-done | bytes 294944 | tf_op jit(solution)/shard_map/ppermute | solution.py:1049
  52.9 13.2 %collective-permute-done.6 = bf16[8,96,512]{2,1,0:T(8,128)(2,1)} collective-permute-done((bf16[8,96,512]{2,1,0:T(8,128)(2,1)}, bf16[8,96,512]{2,1,0:T(8,128)(2,1)}, u32[]{:S(2)}, u32[]{:S(2)}) %collective-permute-start.6) | collective-permute-done | bytes 786464 | tf_op jit(solution)/shard_map/ppermute | solution.py:29
  67.1 3.5 collective-permute-start.11
  73.7 4.2 all-to-all-start.1
  80.1 21.0 %attend.1 = (bf16[4,192,512]{2,1,0:T(8,128)(2,1)}, f32[3,1,2048]{2,1,0:T(1,128)S(1)}, bf16[576,2048]{1,0:T(8,128)(2,1)}, bf16[576,768]{1,0:T(8,128)(2,1)}) custom-call(s32[8]{0:T(128)S(1)} %concatenate.22.scalars, bf16[512,768]{1,0:T(8,128)(2,1)S(1)} %multiply_convert_fusion.1.refs_0_.refs_2_, bf16[512,768]{1,0:T(8,128)(2,1)S(1)} %collective-permute-done.1.refs_1_.refs_3_, ...), custom_call_target="tpu_custom_call" | custom-call | flops 27599998976 | bytes 65536 | tf_op jit(solution)/shard_map/attend/pallas_call | solution.py:152
  105.1 3.8 all-to-all-start.2
  108.9 3.3 maximum_select_fusion
  112.2 4.3 pick.2
  119.4 4.2 collective-permute-done.13.refs_3_
  123.6 4.5 all-to-all-start.3
  131.7 5.8 %middle.1 = (f32[512,768]{1,0:T(8,128)}, bf16[512,896]{1,0:T(8,128)(2,1)}, f32[512,128]{1,0:T(8,128)S(1)}) custom-call(s32[8]{0:T(128)S(1)} %concatenate.22.scalars, bf16[4,192,512]{2,1,0:T(8,128)(2,1)S(1)} %all-to-all-done.2.mixed, bf16[4,2,96,192]{3,2,1,0:T(8,128)(2,1)} %pad_maximum_fusion.1.p0, bf16[4,2,96,192]{3,2,1,0:T(8,128)(2,1)} %collective-permute-done.14.p1, ...), custom_call_target="tpu_custom_call" | custom-call | flops 6899999744 | bytes 65536 | tf_op jit(solution)/shard_map/middle/pallas_call | solution.py:831
  141.2 2.5 collective-permute-start.20
  146.4 14.5 %collective-permute-done.20.refs_4_ = bf16[2,2,96,512]{3,2,1,0:T(8,128)(2,1)S(1)} collective-permute-done((bf16[2,2,96,512]{3,2,1,0:T(8,128)(2,1)S(1)}, bf16[2,2,96,512]{3,2,1,0:T(8,128)(2,1)S(1)}, u32[]{:S(2)}, u32[]{:S(2)}) %collective-permute-start.20) | collective-permute-done | bytes 393248 | tf_op jit(solution)/shard_map/ppermute | solution.py:29
  162.4 6.9 %collective-permute-done.19.refs_17_ = bf16[192,768]{1,0:T(8,128)(2,1)S(1)} collective-permute-done((bf16[192,768]{1,0:T(8,128)(2,1)S(1)}, bf16[192,768]{1,0:T(8,128)(2,1)S(1)}, u32[]{:S(2)}, u32[]{:S(2)}) %collective-permute-start.19) | collective-permute-done | bytes 294944 | tf_op jit(solution)/shard_map/ppermute | solution.py:1049
  173.9 4.9 %pick.3 = (bf16[192,896]{1,0:T(8,128)(2,1)S(1)}, bf16[192,896]{1,0:T(8,128)(2,1)S(1)}, bf16[192,896]{1,0:T(8,128)(2,1)S(1)}, bf16[192,896]{1,0:T(8,128)(2,1)S(1)}) custom-call(s32[8,2048]{1,0:T(8,128)S(1)} %get-tuple-element.175.ids_ref, bf16[512,896]{1,0:T(8,128)(2,1)} %get-tuple-element.188.refs_0_, bf16[512,896]{1,0:T(8,128)(2,1)} %collective-permute-done.21.refs_1_, ...), custom_call_target="tpu_custom_call" | custom-call | flops 5750000128 | bytes 65536 | tf_op jit(solution)/shard_map/pick/pallas_call | solution.py:588
  179.3 2.8 collective-permute-start.33
  184.9 15.2 %collective-permute-done.33.refs_5_ = bf16[2,2,96,512]{3,2,1,0:T(8,128)(2,1)S(1)} collective-permute-done((bf16[2,2,96,512]{3,2,1,0:T(8,128)(2,1)S(1)}, bf16[2,2,96,512]{3,2,1,0:T(8,128)(2,1)S(1)}, u32[]{:S(2)}, u32[]{:S(2)}) %collective-permute-start.33) | collective-permute-done | bytes 393248 | tf_op jit(solution)/shard_map/ppermute | solution.py:29
  203.8 6.9 %collective-permute-done.25.refs_9_ = bf16[192,896]{1,0:T(8,128)(2,1)} collective-permute-done((bf16[192,896]{1,0:T(8,128)(2,1)S(1)}, bf16[192,896]{1,0:T(8,128)(2,1)}, u32[]{:S(2)}, u32[]{:S(2)}) %collective-permute-start.25) | collective-permute-done | bytes 344096 | tf_op jit(solution)/shard_map/ppermute | solution.py:1049
  215.9 35.0 %expert_pass.1 = (f32[768,896]{1,0:T(8,128)}, bf16[768,896]{1,0:T(8,128)(2,1)}, f32[768,768]{1,0:T(8,128)}, bf16[768,768]{1,0:T(8,128)(2,1)}, bf16[2,4,2,3,96,512]{5,4,3,2,1,0:T(8,128)(2,1)}) custom-call(s32[2]{0:T(128)} %pad_add_fusion.scalars, bf16[4,2,2,96,512]{4,3,2,1,0:T(8,128)(2,1)} %bitcast.27.w_gate, bf16[4,2,96,512]{3,2,1,0:T(8,128)(2,1)} %bitcast.19.refs_0_, ...), custom_call_target="tpu_custom_call" | custom-call | flops 40249999360 | bytes 65536 | tf_op jit(solution)/shard_map/expert_pass/pallas_call | solution.py:522
  251.5 2.8 collective-permute-done.35.core_ref
  258.5 2.4 collective-permute-start.38
  260.9 6.9 %collective-permute-done.36.refs_1_ = bf16[192,896]{1,0:T(8,128)(2,1)} collective-permute-done((bf16[192,896]{1,0:T(8,128)(2,1)}, bf16[192,896]{1,0:T(8,128)(2,1)}, u32[]{:S(2)}, u32[]{:S(2)}) %collective-permute-start.36) | collective-permute-done | bytes 344096 | tf_op jit(solution)/shard_map/ppermute | solution.py:1049
  267.8 14.6 %collective-permute-done.38.refs_3_ = bf16[192,896]{1,0:T(8,128)(2,1)} collective-permute-done((bf16[192,896]{1,0:T(8,128)(2,1)}, bf16[192,896]{1,0:T(8,128)(2,1)}, u32[]{:S(2)}, u32[]{:S(2)}) %collective-permute-start.38) | collective-permute-done | bytes 344096 | tf_op jit(solution)/shard_map/ppermute | solution.py:1049
  284.6 5.1 %spread.2 = (f32[2,512,896]{2,1,0:T(8,128)S(1)}, bf16[2,512,896]{2,1,0:T(8,128)(2,1)S(1)}) custom-call(s32[2048,8]{1,0:T(8,128)S(1)} %copy-done.49, bf16[192,896]{1,0:T(8,128)(2,1)S(1)} %copy-done.45, bf16[192,896]{1,0:T(8,128)(2,1)} %collective-permute-done.36.refs_1_, bf16[192,896]{1,0:T(8,128)(2,1)} %collective-permute-done.37.refs_2_, ...), custom_call_target="tpu_custom_call" | custom-call | flops 34500001792 | bytes 65536 | tf_op jit(solution)/shard_map/spread/pallas_call | solution.py:693
  291.6 3.4 collective-permute-done.40.got_ref
  304.7 13.9 %collective-permute-done.41.far_ref = bf16[512,896]{1,0:T(8,128)(2,1)S(1)} collective-permute-done((bf16[512,896]{1,0:T(8,128)(2,1)}, bf16[512,896]{1,0:T(8,128)(2,1)S(1)}, u32[]{:S(2)}, u32[]{:S(2)}) %collective-permute-start.41) | collective-permute-done | bytes 917536 | tf_op jit(solution)/shard_map/ppermute | solution.py:29
  320.7 8.9 %router_back.1 = (f32[512,768]{1,0:T(8,128)}, bf16[512,768]{1,0:T(8,128)(2,1)S(1)}, f32[512,768]{1,0:T(8,128)}, f32[512,12]{1,0:T(8,128)S(1)}, f32[32,768]{1,0:T(8,128)S(1)}) custom-call(s32[8]{0:T(128)S(1)} %concatenate.22.scalars, f32[2,512,896]{2,1,0:T(8,128)} %copy-done.1, bf16[2,512,896]{2,1,0:T(8,128)(2,1)} %copy-done.58, ...), custom_call_target="tpu_custom_call" | custom-call | flops 9200000000 | bytes 65536 | tf_op jit(solution)/shard_map/router_back/pallas_call | solution.py:996
  329.7 3.1 mixed_back.1
  339.1 4.0 all-to-all-start.4
  343.1 2.4 collective-permute-start.47
  353.5 23.2 %attend_back.1 = bf16[4,3,192,512]{3,2,1,0:T(8,128)(2,1)S(1)} custom-call(s32[8]{0:T(128)S(1)} %concatenate.22.scalars, bf16[576,2048]{1,0:T(8,128)(2,1)S(1)} %copy-done.55, f32[3,1,2048]{2,1,0:T(1,128)S(1)} %get-tuple-element.252.lse_ref, bf16[192,512]{1,0:T(8,128)(2,1)S(1)} %copy-done.52, bf16[192,512]{1,0:T(8,128)(2,1)S(1)} %collective-permute-done.42.refs_1_, ...), custom_call_target="tpu_custom_call" | custom-call | flops 39099998208 | bytes 65536 | tf_op jit(solution)/shard_map/attend_back/pallas_call | solution.py:294
  376.8 2.3 collective-permute-done.47.refs_3_
  384.5 4.9 %spread.3 = (f32[2,512,768]{2,1,0:T(8,128)S(1)}, bf16[2,512,768]{2,1,0:T(8,128)(2,1)}) custom-call(s32[2048,8]{1,0:T(8,128)S(1)} %copy-done.50, bf16[192,768]{1,0:T(8,128)(2,1)S(1)} %copy-done.47, bf16[192,768]{1,0:T(8,128)(2,1)S(1)} %copy-done.28, bf16[192,768]{1,0:T(8,128)(2,1)} %collective-permute-done.46.refs_2_, bf16[192,768]{1,0:T(8,128)(2,1)S(1)} %copy-done.36), custom_call_target="tpu_custom_call" | custom-call | flops 34500001792 | bytes 65536 | tf_op jit(solution)/shard_map/spread/pallas_call | solution.py:693
  389.8 4.4 all-to-all-start.5
  397.6 6.9 %attn_grads.1 = (bf16[4,96,768]{2,1,0:T(8,128)(2,1)S(1)}, bf16[4,96,768]{2,1,0:T(8,128)(2,1)}) custom-call(s32[8]{0:T(128)S(1)} %concatenate.22.scalars, bf16[4,576,512]{2,1,0:T(8,128)(2,1)} %bitcast.96, bf16[4,192,512]{2,1,0:T(8,128)(2,1)} %get-tuple-element.174.refs_1_, bf16[512,768]{1,0:T(8,128)(2,1)S(1)} %copy-done.3, bf16[512,768]{1,0:T(8,128)(2,1)S(1)} %copy-done.21, ...), custom_call_target="tpu_custom_call" | custom-call | flops 34500001792 | bytes 65536 | tf_op jit(solution)/shard_map/attn_grads/pallas_call | solution.py:208
  407.0 2.2 fusion.3
  409.3 13.9 %collective-permute-done.51.g3 = bf16[576,512]{1,0:T(8,128)(2,1)} collective-permute-done((bf16[576,512]{1,0:T(8,128)(2,1)}, bf16[576,512]{1,0:T(8,128)(2,1)}, u32[]{:S(2)}, u32[]{:S(2)}) %collective-permute-start.51) | collective-permute-done | bytes 589856 | tf_op jit(solution)/shard_map/ppermute | solution.py:606
  423.2 13.6 %collective-permute-done.54 = bf16[4,96,768]{2,1,0:T(8,128)(2,1)} collective-permute-done((bf16[4,96,768]{2,1,0:T(8,128)(2,1)}, bf16[4,96,768]{2,1,0:T(8,128)(2,1)}, u32[]{:S(2)}, u32[]{:S(2)}) %collective-permute-start.54) | collective-permute-done | bytes 589856 | tf_op jit(solution)/shard_map/ppermute | solution.py:29
  436.8 2.3 fusion.9
  439.8 3.6 collective-permute-start.59
  443.7 6.7 %inputs_back.1 = (f32[512,768]{1,0:T(8,128)}, f32[2,1,768]{2,1,0:T(1,128)S(1)}) custom-call(bf16[576,512]{1,0:T(8,128)(2,1)S(1)} %copy-done.5, bf16[576,512]{1,0:T(8,128)(2,1)} %collective-permute-done.49.g1, bf16[576,512]{1,0:T(8,128)(2,1)} %collective-permute-done.50.g2, bf16[576,512]{1,0:T(8,128)(2,1)} %collective-permute-done.51.g3, ...), custom_call_target="tpu_custom_call" | custom-call | flops 6899999744 | bytes 65536 | tf_op jit(solution)/shard_map/inputs_back/pallas_call | solution.py:376
  453.0 6.2 %all-to-all-start.6 = ((f32[32,1,1536]{2,1,0:T(1,128)}), f32[32,1,1536]{2,1,0:T(1,128)}, u32[]{:S(2)}, u32[]{:S(2)}) async-start(f32[32,1,1536]{2,1,0:T(1,128)} %broadcast_in_dim.5), calls=%async_computation.7 | async-start | bytes 393216 | tf_op jit(solution)/shard_map/all_to_all | solution.py:1045
  459.3 3.3 fusion.1
  462.6 4.0 convert_bitcast_fusion
  (332 shorter events, 118.0 us)
Async XLA Ops:
  9.8 17.4 %collective-permute-start = (bf16[96,768]{1,0:T(8,128)(2,1)}, bf16[96,768]{1,0:T(8,128)(2,1)}, u32[]{:S(2)}, u32[]{:S(2)}) collective-permute-start(bf16[96,768]{1,0:T(8,128)(2,1)} %pad_maximum_fusion.3), channel_id=1, source_target_pairs={{0,16},{16,0},{1,17},{17,1},{2,18},{18,2},{3,19},{19,3},{4,20},{20... | collective-permute-start | bytes 442376 | tf_op jit(solution)/shard_map/ppermute | solution.py:29
  14.8 38.0 %collective-permute-start.2 = (bf16[512,768]{1,0:T(8,128)(2,1)S(1)}, bf16[512,768]{1,0:T(8,128)(2,1)}, u32[]{:S(2)}, u32[]{:S(2)}) collective-permute-start(bf16[512,768]{1,0:T(8,128)(2,1)S(1)} %multiply_convert_fusion.1.refs_0_.refs_2_), channel_id=1, source_target_pairs={{0,2},{2,0},{1,3},{3,1},{4,6},{6,4},{5,7},{7,5},{8,10},{10,8},{9,1... | collective-permute-start | bytes 2359304 | tf_op jit(solution)/shard_map/ppermute | solution.py:29
  16.1 50.0 %all-to-all-start = ((bf16[8,96,512]{2,1,0:T(8,128)(2,1)}), bf16[8,96,512]{2,1,0:T(8,128)(2,1)}, u32[]{:S(2)}, u32[]{:S(2)}) async-start(bf16[8,96,512]{2,1,0:T(8,128)(2,1)} %param.36), calls=%async_computation | async-start | bytes 1572864 | tf_op jit(solution)/shard_map/all_to_all | solution.py:1147
  28.3 13.7 %collective-permute-start.3 = (bf16[2,96,768]{2,1,0:T(8,128)(2,1)S(1)}, bf16[2,96,768]{2,1,0:T(8,128)(2,1)}, u32[]{:S(2)}, u32[]{:S(2)}) collective-permute-start(bf16[2,96,768]{2,1,0:T(8,128)(2,1)S(1)} %pad_maximum_fusion.2.refs_4_), channel_id=1, source_target_pairs={{0,4},{4,0},{8,12},{12,8},{1,5},{5,1},{9,13},{13,9},{2,6},{6,2},{1... | collective-permute-start | bytes 884744 | tf_op jit(solution)/shard_map/ppermute | solution.py:1049
  29.6 15.9 %collective-permute-start.4 = (bf16[2,96,768]{2,1,0:T(8,128)(2,1)S(1)}, bf16[2,96,768]{2,1,0:T(8,128)(2,1)}, u32[]{:S(2)}, u32[]{:S(2)}) collective-permute-start(bf16[2,96,768]{2,1,0:T(8,128)(2,1)S(1)} %pad_maximum_fusion.2.refs_4_), channel_id=1, source_target_pairs={{0,8},{4,12},{8,0},{12,4},{1,9},{5,13},{9,1},{13,5},{2,10},{6,14},... | collective-permute-start | bytes 884744 | tf_op jit(solution)/shard_map/ppermute | solution.py:1049
  30.8 22.0 %collective-permute-start.5 = (bf16[2,96,768]{2,1,0:T(8,128)(2,1)S(1)}, bf16[2,96,768]{2,1,0:T(8,128)(2,1)}, u32[]{:S(2)}, u32[]{:S(2)}) collective-permute-start(bf16[2,96,768]{2,1,0:T(8,128)(2,1)S(1)} %pad_maximum_fusion.2.refs_4_), channel_id=1, source_target_pairs={{0,12},{4,8},{8,4},{12,0},{1,13},{5,9},{9,5},{13,1},{2,14},{6,10},... | collective-permute-start | bytes 884744 | tf_op jit(solution)/shard_map/ppermute | solution.py:1049
  31.0 35.1 %collective-permute-start.6 = (bf16[8,96,512]{2,1,0:T(8,128)(2,1)}, bf16[8,96,512]{2,1,0:T(8,128)(2,1)}, u32[]{:S(2)}, u32[]{:S(2)}) collective-permute-start(bf16[8,96,512]{2,1,0:T(8,128)(2,1)} %param.35), channel_id=1, source_target_pairs={{0,16},{16,0},{1,17},{17,1},{2,18},{18,2},{3,19},{19,3},{4,20},{20... | collective-permute-start | bytes 2359304 | tf_op jit(solution)/shard_map/ppermute | solution.py:29
  42.0 37.9 %collective-permute-start.1 = (bf16[512,768]{1,0:T(8,128)(2,1)S(1)}, bf16[512,768]{1,0:T(8,128)(2,1)S(1)}, u32[]{:S(2)}, u32[]{:S(2)}) collective-permute-start(bf16[512,768]{1,0:T(8,128)(2,1)S(1)} %multiply_convert_fusion.1.refs_0_.refs_2_), channel_id=1, source_target_pairs={{0,1},{1,0},{2,3},{3,2},{4,5},{5,4},{6,7},{7,6},{8,9},{9,8},{10,11... | collective-permute-start | bytes 2359304 | tf_op jit(solution)/shard_map/ppermute | solution.py:29
  66.1 35.8 %collective-permute-start.10 = (bf16[512,768]{1,0:T(8,128)(2,1)}, bf16[512,768]{1,0:T(8,128)(2,1)}, u32[]{:S(2)}, u32[]{:S(2)}) collective-permute-start(bf16[512,768]{1,0:T(8,128)(2,1)} %multiply_convert_fusion.refs_0_), channel_id=1, source_target_pairs={{0,2},{2,0},{1,3},{3,1},{4,6},{6,4},{5,7},{7,5},{8,10},{10,8},{9,1... | collective-permute-start | bytes 2359304 | tf_op jit(solution)/shard_map/ppermute | solution.py:29
  67.1 45.1 %collective-permute-start.11 = (bf16[512,768]{1,0:T(8,128)(2,1)}, bf16[512,768]{1,0:T(8,128)(2,1)}, u32[]{:S(2)}, u32[]{:S(2)}) collective-permute-start(bf16[512,768]{1,0:T(8,128)(2,1)} %multiply_convert_fusion.refs_0_), channel_id=1, source_target_pairs={{0,1},{1,0},{2,3},{3,2},{4,5},{5,4},{6,7},{7,6},{8,9},{9,8},{10,11... | collective-permute-start | bytes 2359304 | tf_op jit(solution)/shard_map/ppermute | solution.py:29
  73.6 27.5 %collective-permute-start.8 = (bf16[4,2,96,192]{3,2,1,0:T(8,128)(2,1)}, bf16[4,2,96,192]{3,2,1,0:T(8,128)(2,1)}, u32[]{:S(2)}, u32[]{:S(2)}) collective-permute-start(bf16[4,2,96,192]{3,2,1,0:T(8,128)(2,1)} %pad_maximum_fusion.1.p0), channel_id=1, source_target_pairs={{0,2},{2,0},{1,3},{3,1},{4,6},{6,4},{5,7},{7,5},{8,10},{10,8},{9,1... | collective-permute-start | bytes 884744 | tf_op jit(solution)/shard_map/ppermute | solution.py:29
  73.7 28.2 %all-to-all-start.1 = ((bf16[8,96,512]{2,1,0:T(8,128)(2,1)}), bf16[8,96,512]{2,1,0:T(8,128)(2,1)}, u32[]{:S(2)}, u32[]{:S(2)}) async-start(bf16[8,96,512]{2,1,0:T(8,128)(2,1)} %bitcast.101), calls=%async_computation.1 | async-start | bytes 1572864 | tf_op jit(solution)/shard_map/all_to_all | solution.py:1177
  79.9 21.2 %collective-permute-start.9 = (bf16[2,2,96,512]{3,2,1,0:T(8,128)(2,1)S(1)}, bf16[2,2,96,512]{3,2,1,0:T(8,128)(2,1)S(1)}, u32[]{:S(2)}, u32[]{:S(2)}) collective-permute-start(bf16[2,2,96,512]{3,2,1,0:T(8,128)(2,1)S(1)} %get-tuple-element.346), channel_id=1, source_target_pairs={{0,16},{16,0},{1,17},{17,1},{2,18},{18,2},{3,19},{19,3},{4,20},{20... | collective-permute-start | bytes 1179656 | tf_op jit(solution)/shard_map/ppermute | solution.py:29
  103.3 20.3 %collective-permute-start.13 = (bf16[2,2,96,512]{3,2,1,0:T(8,128)(2,1)}, bf16[2,2,96,512]{3,2,1,0:T(8,128)(2,1)}, u32[]{:S(2)}, u32[]{:S(2)}) collective-permute-start(bf16[2,2,96,512]{3,2,1,0:T(8,128)(2,1)} %get-tuple-element.345), channel_id=1, source_target_pairs={{0,16},{16,0},{1,17},{17,1},{2,18},{18,2},{3,19},{19,3},{4,20},{20... | collective-permute-start | bytes 1179656 | tf_op jit(solution)/shard_map/ppermute | solution.py:29
  105.1 18.5 %all-to-all-start.2 = ((bf16[4,192,512]{2,1,0:T(8,128)(2,1)}), bf16[4,192,512]{2,1,0:T(8,128)(2,1)S(1)}, u32[]{:S(2)}, u32[]{:S(2)}) async-start(bf16[4,192,512]{2,1,0:T(8,128)(2,1)} %get-tuple-element.174.refs_1_), calls=%async_computation.2 | async-start | bytes 1572864 | tf_op jit(solution)/shard_map/all_to_all | solution.py:1204
  123.6 46.4 %all-to-all-start.3 = ((bf16[8,2,96,512]{3,2,1,0:T(8,128)(2,1)}), bf16[8,2,96,512]{3,2,1,0:T(8,128)(2,1)}, u32[]{:S(2)}, u32[]{:S(2)}) async-start(bf16[8,2,96,512]{3,2,1,0:T(8,128)(2,1)} %maximum_select_fusion), calls=%async_computation.3 | async-start | bytes 3145728 | tf_op jit(solution)/shard_map/all_to_all | solution.py:1217
  128.1 251.7 %reduce-scatter.2.cloned.1.call-start = ((), (), s32[]{:S(2)}) async-start(), calls=%async_computation.8 | async-start | bytes 7077888 | tf_op jit(solution)/shard_map/reduce_scatter | solution.py:1071
  137.6 32.5 %collective-permute-start.16 = (bf16[512,896]{1,0:T(8,128)(2,1)}, bf16[512,896]{1,0:T(8,128)(2,1)S(1)}, u32[]{:S(2)}, u32[]{:S(2)}) collective-permute-start(bf16[512,896]{1,0:T(8,128)(2,1)} %get-tuple-element.188.refs_0_), channel_id=1, source_target_pairs={{0,2},{2,0},{1,3},{3,1},{4,6},{6,4},{5,7},{7,5},{8,10},{10,8},{9,1... | collective-permute-start | bytes 2752520 | tf_op jit(solution)/shard_map/ppermute | solution.py:29
  141.2 19.7 %collective-permute-start.20 = (bf16[2,2,96,512]{3,2,1,0:T(8,128)(2,1)S(1)}, bf16[2,2,96,512]{3,2,1,0:T(8,128)(2,1)S(1)}, u32[]{:S(2)}, u32[]{:S(2)}) collective-permute-start(bf16[2,2,96,512]{3,2,1,0:T(8,128)(2,1)S(1)} %get-tuple-element.344), channel_id=1, source_target_pairs={{0,16},{16,0},{1,17},{17,1},{2,18},{18,2},{3,19},{19,3},{4,20},{20... | collective-permute-start | bytes 1179656 | tf_op jit(solution)/shard_map/ppermute | solution.py:29
  143.7 18.6 %collective-permute-start.17 = (bf16[192,768]{1,0:T(8,128)(2,1)S(1)}, bf16[192,768]{1,0:T(8,128)(2,1)S(1)}, u32[]{:S(2)}, u32[]{:S(2)}) collective-permute-start(bf16[192,768]{1,0:T(8,128)(2,1)S(1)} %copy-done.34), channel_id=1, source_target_pairs={{0,4},{4,0},{8,12},{12,8},{1,5},{5,1},{9,13},{13,9},{2,6},{6,2},{1... | collective-permute-start | bytes 884744 | tf_op jit(solution)/shard_map/ppermute | solution.py:1049
  144.9 17.5 %collective-permute-start.18 = (bf16[192,768]{1,0:T(8,128)(2,1)S(1)}, bf16[192,768]{1,0:T(8,128)(2,1)S(1)}, u32[]{:S(2)}, u32[]{:S(2)}) collective-permute-start(bf16[192,768]{1,0:T(8,128)(2,1)S(1)} %copy-done.32), channel_id=1, source_target_pairs={{0,8},{4,12},{8,0},{12,4},{1,9},{5,13},{9,1},{13,5},{2,10},{6,14},... | collective-permute-start | bytes 884744 | tf_op jit(solution)/shard_map/ppermute | solution.py:1049
  146.1 23.2 %collective-permute-start.19 = (bf16[192,768]{1,0:T(8,128)(2,1)S(1)}, bf16[192,768]{1,0:T(8,128)(2,1)S(1)}, u32[]{:S(2)}, u32[]{:S(2)}) collective-permute-start(bf16[192,768]{1,0:T(8,128)(2,1)S(1)} %copy-done.30), channel_id=1, source_target_pairs={{0,12},{4,8},{8,4},{12,0},{1,13},{5,9},{9,5},{13,1},{2,14},{6,10},... | collective-permute-start | bytes 884744 | tf_op jit(solution)/shard_map/ppermute | solution.py:1049
  160.9 10.9 %collective-permute-start.21 = (bf16[512,896]{1,0:T(8,128)(2,1)}, bf16[512,896]{1,0:T(8,128)(2,1)}, u32[]{:S(2)}, u32[]{:S(2)}) collective-permute-start(bf16[512,896]{1,0:T(8,128)(2,1)} %get-tuple-element.188.refs_0_), channel_id=1, source_target_pairs={{0,1},{1,0},{2,3},{3,2},{4,5},{5,4},{6,7},{7,6},{8,9},{9,8},{10,11... | collective-permute-start | bytes 2752520 | tf_op jit(solution)/shard_map/ppermute | solution.py:29
  178.8 22.0 %collective-permute-start.31 = (bf16[576,768]{1,0:T(8,128)(2,1)}, bf16[576,768]{1,0:T(8,128)(2,1)S(1)}, u32[]{:S(2)}, u32[]{:S(2)}) collective-permute-start(bf16[576,768]{1,0:T(8,128)(2,1)} %get-tuple-element.286.p0), channel_id=1, source_target_pairs={{0,2},{2,0},{1,3},{3,1},{4,6},{6,4},{5,7},{7,5},{8,10},{10,8},{9,1... | collective-permute-start | bytes 2654216 | tf_op jit(solution)/shard_map/ppermute | solution.py:29
  179.3 20.8 %collective-permute-start.33 = (bf16[2,2,96,512]{3,2,1,0:T(8,128)(2,1)S(1)}, bf16[2,2,96,512]{3,2,1,0:T(8,128)(2,1)S(1)}, u32[]{:S(2)}, u32[]{:S(2)}) collective-permute-start(bf16[2,2,96,512]{3,2,1,0:T(8,128)(2,1)S(1)} %copy-done.59), channel_id=1, source_target_pairs={{0,16},{16,0},{1,17},{17,1},{2,18},{18,2},{3,19},{19,3},{4,20},{20... | collective-permute-start | bytes 1179656 | tf_op jit(solution)/shard_map/ppermute | solution.py:29
  182.1 18.0 %collective-permute-start.23 = (bf16[192,896]{1,0:T(8,128)(2,1)S(1)}, bf16[192,896]{1,0:T(8,128)(2,1)S(1)}, u32[]{:S(2)}, u32[]{:S(2)}) collective-permute-start(bf16[192,896]{1,0:T(8,128)(2,1)S(1)} %get-tuple-element.206), channel_id=1, source_target_pairs={{0,4},{4,0},{8,12},{12,8},{1,5},{5,1},{9,13},{13,9},{2,6},{6,2},{1... | collective-permute-start | bytes 1032200 | tf_op jit(solution)/shard_map/ppermute | solution.py:1049
  183.5 32.4 %collective-permute-start.34 = (bf16[768,768]{1,0:T(8,128)(2,1)}, bf16[768,768]{1,0:T(8,128)(2,1)}, u32[]{:S(2)}, u32[]{:S(2)}) collective-permute-start(bf16[768,768]{1,0:T(8,128)(2,1)} %pad_maximum_fusion), channel_id=1, source_target_pairs={{0,1},{1,0},{2,3},{3,2},{4,5},{5,4},{6,7},{7,6},{8,9},{9,8},{10,11... | collective-permute-start | bytes 3538952 | tf_op jit(solution)/shard_map/ppermute | solution.py:29
  184.7 18.1 %collective-permute-start.24 = (bf16[192,896]{1,0:T(8,128)(2,1)S(1)}, bf16[192,896]{1,0:T(8,128)(2,1)}, u32[]{:S(2)}, u32[]{:S(2)}) collective-permute-start(bf16[192,896]{1,0:T(8,128)(2,1)S(1)} %get-tuple-element.207), channel_id=1, source_target_pairs={{0,8},{4,12},{8,0},{12,4},{1,9},{5,13},{9,1},{13,5},{2,10},{6,14},... | collective-permute-start | bytes 1032200 | tf_op jit(solution)/shard_map/ppermute | solution.py:1049
  200.1 15.8 %collective-permute-start.30 = (bf16[576,768]{1,0:T(8,128)(2,1)}, bf16[576,768]{1,0:T(8,128)(2,1)}, u32[]{:S(2)}, u32[]{:S(2)}) collective-permute-start(bf16[576,768]{1,0:T(8,128)(2,1)} %get-tuple-element.286.p0), channel_id=1, source_target_pairs={{0,1},{1,0},{2,3},{3,2},{4,5},{5,4},{6,7},{7,6},{8,9},{9,8},{10,11... | collective-permute-start | bytes 2654216 | tf_op jit(solution)/shard_map/ppermute | solution.py:29
  200.8 15.1 %collective-permute-start.32 = (bf16[576,768]{1,0:T(8,128)(2,1)S(1)}, bf16[576,768]{1,0:T(8,128)(2,1)}, u32[]{:S(2)}, u32[]{:S(2)}) collective-permute-start(bf16[576,768]{1,0:T(8,128)(2,1)S(1)} %collective-permute-done.31.p2), channel_id=1, source_target_pairs={{0,1},{1,0},{2,3},{3,2},{4,5},{5,4},{6,7},{7,6},{8,9},{9,8},{10,11... | collective-permute-start | bytes 2654216 | tf_op jit(solution)/shard_map/ppermute | solution.py:29
  258.5 23.9 %collective-permute-start.38 = (bf16[192,896]{1,0:T(8,128)(2,1)}, bf16[192,896]{1,0:T(8,128)(2,1)}, u32[]{:S(2)}, u32[]{:S(2)}) collective-permute-start(bf16[192,896]{1,0:T(8,128)(2,1)} %get-tuple-element.228), channel_id=1, source_target_pairs={{0,12},{4,8},{8,4},{12,0},{1,13},{5,9},{9,5},{13,1},{2,14},{6,10},... | collective-permute-start | bytes 1032200 | tf_op jit(solution)/shard_map/ppermute | solution.py:1049
  296.6 22.0 %collective-permute-start.41 = (bf16[512,896]{1,0:T(8,128)(2,1)}, bf16[512,896]{1,0:T(8,128)(2,1)S(1)}, u32[]{:S(2)}, u32[]{:S(2)}) collective-permute-start(bf16[512,896]{1,0:T(8,128)(2,1)} %fusion.2), channel_id=1, source_target_pairs={{0,2},{2,0},{1,3},{3,1},{4,6},{6,4},{5,7},{7,5},{8,10},{10,8},{9,1... | collective-permute-start | bytes 2752520 | tf_op jit(solution)/shard_map/ppermute | solution.py:29
  334.5 11.0 %collective-permute-start.43 = (bf16[192,512]{1,0:T(8,128)(2,1)S(1)}, bf16[192,512]{1,0:T(8,128)(2,1)S(1)}, u32[]{:S(2)}, u32[]{:S(2)}) collective-permute-start(bf16[192,512]{1,0:T(8,128)(2,1)S(1)} %get-tuple-element.256), channel_id=1, source_target_pairs={{0,2},{1,3},{2,0},{3,1},{4,6},{5,7},{6,4},{7,5},{8,10},{9,11},{10,... | collective-permute-start | bytes 589832 | tf_op jit(solution)/shard_map/ppermute | solution.py:606
  336.1 40.6 %collective-permute-start.45 = (bf16[192,768]{1,0:T(8,128)(2,1)}, bf16[192,768]{1,0:T(8,128)(2,1)S(1)}, u32[]{:S(2)}, u32[]{:S(2)}) collective-permute-start(bf16[192,768]{1,0:T(8,128)(2,1)} %get-tuple-element.263), channel_id=1, source_target_pairs={{0,4},{4,0},{8,12},{12,8},{1,5},{5,1},{9,13},{13,9},{2,6},{6,2},{1... | collective-permute-start | bytes 884744 | tf_op jit(solution)/shard_map/ppermute | solution.py:1049
  336.4 40.3 %collective-permute-start.46 = (bf16[192,768]{1,0:T(8,128)(2,1)}, bf16[192,768]{1,0:T(8,128)(2,1)}, u32[]{:S(2)}, u32[]{:S(2)}) collective-permute-start(bf16[192,768]{1,0:T(8,128)(2,1)} %get-tuple-element.264), channel_id=1, source_target_pairs={{0,8},{4,12},{8,0},{12,4},{1,9},{5,13},{9,1},{13,5},{2,10},{6,14},... | collective-permute-start | bytes 884744 | tf_op jit(solution)/shard_map/ppermute | solution.py:1049
  339.1 50.8 %all-to-all-start.4 = ((f32[32,1,768]{2,1,0:T(1,128)}), f32[32,1,768]{2,1,0:T(1,128)}, u32[]{:S(2)}, u32[]{:S(2)}) async-start(f32[32,1,768]{2,1,0:T(1,128)} %copy.58), calls=%async_computation.5 | async-start | bytes 196608 | tf_op jit(solution)/shard_map/all_to_all | solution.py:1260
  343.1 35.9 %collective-permute-start.47 = (bf16[192,768]{1,0:T(8,128)(2,1)S(1)}, bf16[192,768]{1,0:T(8,128)(2,1)S(1)}, u32[]{:S(2)}, u32[]{:S(2)}) collective-permute-start(bf16[192,768]{1,0:T(8,128)(2,1)S(1)} %copy-done.26), channel_id=1, source_target_pairs={{0,12},{4,8},{8,4},{12,0},{1,13},{5,9},{9,5},{13,1},{2,14},{6,10},... | collective-permute-start | bytes 884744 | tf_op jit(solution)/shard_map/ppermute | solution.py:1049
  346.9 32.8 %collective-permute-start.48 = (bf16[512,768]{1,0:T(8,128)(2,1)}, bf16[512,768]{1,0:T(8,128)(2,1)}, u32[]{:S(2)}, u32[]{:S(2)}) collective-permute-start(bf16[512,768]{1,0:T(8,128)(2,1)} %copy-done.22), channel_id=1, source_target_pairs={{0,2},{2,0},{1,3},{3,1},{4,6},{6,4},{5,7},{7,5},{8,10},{10,8},{9,1... | collective-permute-start | bytes 2359304 | tf_op jit(solution)/shard_map/ppermute | solution.py:29
  348.1 41.3 %collective-permute-start.52 = (bf16[512,768]{1,0:T(8,128)(2,1)}, bf16[512,768]{1,0:T(8,128)(2,1)}, u32[]{:S(2)}, u32[]{:S(2)}) collective-permute-start(bf16[512,768]{1,0:T(8,128)(2,1)} %copy-done.22), channel_id=1, source_target_pairs={{0,1},{1,0},{2,3},{3,2},{4,5},{5,4},{6,7},{7,6},{8,9},{9,8},{10,11... | collective-permute-start | bytes 2359304 | tf_op jit(solution)/shard_map/ppermute | solution.py:29
  381.2 28.0 %collective-permute-start.49 = (bf16[576,512]{1,0:T(8,128)(2,1)}, bf16[576,512]{1,0:T(8,128)(2,1)}, u32[]{:S(2)}, u32[]{:S(2)}) collective-permute-start(bf16[576,512]{1,0:T(8,128)(2,1)} %get-tuple-element.339), channel_id=1, source_target_pairs={{0,1},{1,0},{2,3},{3,2},{4,5},{5,4},{6,7},{7,6},{8,9},{9,8},{10,11... | collective-permute-start | bytes 1769480 | tf_op jit(solution)/shard_map/ppermute | solution.py:606
  381.7 27.6 %collective-permute-start.50 = (bf16[576,512]{1,0:T(8,128)(2,1)}, bf16[576,512]{1,0:T(8,128)(2,1)}, u32[]{:S(2)}, u32[]{:S(2)}) collective-permute-start(bf16[576,512]{1,0:T(8,128)(2,1)} %get-tuple-element.338), channel_id=1, source_target_pairs={{0,2},{1,3},{2,0},{3,1},{4,6},{5,7},{6,4},{7,5},{8,10},{9,11},{10,... | collective-permute-start | bytes 1769480 | tf_op jit(solution)/shard_map/ppermute | solution.py:606
  382.9 40.3 %collective-permute-start.51 = (bf16[576,512]{1,0:T(8,128)(2,1)}, bf16[576,512]{1,0:T(8,128)(2,1)}, u32[]{:S(2)}, u32[]{:S(2)}) collective-permute-start(bf16[576,512]{1,0:T(8,128)(2,1)} %get-tuple-element.337), channel_id=1, source_target_pairs={{0,3},{1,2},{2,1},{3,0},{4,7},{5,6},{6,5},{7,4},{8,11},{9,10},{10,... | collective-permute-start | bytes 1769480 | tf_op jit(solution)/shard_map/ppermute | solution.py:606
  383.4 10.8 %collective-permute-start.53 = (bf16[512,768]{1,0:T(8,128)(2,1)}, bf16[512,768]{1,0:T(8,128)(2,1)}, u32[]{:S(2)}, u32[]{:S(2)}) collective-permute-start(bf16[512,768]{1,0:T(8,128)(2,1)} %collective-permute-done.48.refs_8_), channel_id=1, source_target_pairs={{0,1},{1,0},{2,3},{3,2},{4,5},{5,4},{6,7},{7,6},{8,9},{9,8},{10,11... | collective-permute-start | bytes 2359304 | tf_op jit(solution)/shard_map/ppermute | solution.py:29
  389.5 17.5 %collective-permute-start.55 = (bf16[2,512,768]{2,1,0:T(8,128)(2,1)}, bf16[2,512,768]{2,1,0:T(8,128)(2,1)}, u32[]{:S(2)}, u32[]{:S(2)}) collective-permute-start(bf16[2,512,768]{2,1,0:T(8,128)(2,1)} %get-tuple-element.278), channel_id=1, source_target_pairs={{0,1},{1,0},{2,3},{3,2},{4,5},{5,4},{6,7},{7,6},{8,9},{9,8},{10,11... | collective-permute-start | bytes 4718600 | tf_op jit(solution)/shard_map/ppermute | solution.py:29
  389.8 62.4 %all-to-all-start.5 = ((bf16[8,3,96,512]{3,2,1,0:T(8,128)(2,1)}), bf16[8,3,96,512]{3,2,1,0:T(8,128)(2,1)}, u32[]{:S(2)}, u32[]{:S(2)}) async-start(bf16[8,3,96,512]{3,2,1,0:T(8,128)(2,1)} %bitcast.100), calls=%async_computation.6 | async-start | bytes 4718592 | tf_op jit(solution)/shard_map/all_to_all | solution.py:1269
  405.3 31.4 %collective-permute-start.54 = (bf16[4,96,768]{2,1,0:T(8,128)(2,1)}, bf16[4,96,768]{2,1,0:T(8,128)(2,1)}, u32[]{:S(2)}, u32[]{:S(2)}) collective-permute-start(bf16[4,96,768]{2,1,0:T(8,128)(2,1)} %get-tuple-element.272), channel_id=1, source_target_pairs={{0,16},{16,0},{1,17},{17,1},{2,18},{18,2},{3,19},{19,3},{4,20},{20... | collective-permute-start | bytes 1769480 | tf_op jit(solution)/shard_map/ppermute | solution.py:29
  436.8 22.5 %collective-permute-start.56 = (bf16[512,768]{1,0:T(8,128)(2,1)}, bf16[512,768]{1,0:T(8,128)(2,1)}, u32[]{:S(2)}, u32[]{:S(2)}) collective-permute-start(bf16[512,768]{1,0:T(8,128)(2,1)} %fusion.3), channel_id=1, source_target_pairs={{0,2},{2,0},{1,3},{3,1},{4,6},{6,4},{5,7},{7,5},{8,10},{10,8},{9,1... | collective-permute-start | bytes 2359304 | tf_op jit(solution)/shard_map/ppermute | solution.py:29
  453.0 15.5 %all-to-all-start.6 = ((f32[32,1,1536]{2,1,0:T(1,128)}), f32[32,1,1536]{2,1,0:T(1,128)}, u32[]{:S(2)}, u32[]{:S(2)}) async-start(f32[32,1,1536]{2,1,0:T(1,128)} %broadcast_in_dim.5), calls=%async_computation.7 | async-start | bytes 393216 | tf_op jit(solution)/shard_map/all_to_all | solution.py:1045
  (104 other events, 744.0 us)
Sparse Core Ops, SparseCore 0:
  261.0 112.6 reduce-scatter.1
where the time goes:
time: 492 us; the launch traced here: 482 us
  waiting for transfers between devices  150 us (30%)
  Pallas kernels  142 us (29%)
  starting transfers between devices  91.8 us (19%)
  local copies, waits for them, and re-layouts  53.4 us (11%)
  other arithmetic  28.9 us (6%)
  between operations  15.3 us (3%)
    ppermute x36, waiting for transfers between devices, swap(): return lax.ppermute(value, axis, [(0, 1), (1, 0)])  86.1 us
    ppermute x18, waiting for transfers between devices, flip(): return lax.ppermute(value, axis, [(i, i ^ bit) for i in range(size)])  48.3 us
    ppermute x36, starting transfers between devices, swap(): return lax.ppermute(value, axis, [(0, 1), (1, 0)])  38.2 us
    unnamed x176, local copies, waits for them, and re-layouts  35.9 us
    pallas_call x1, Pallas kernels, expert_pass(): pl.pallas_call(functools.partial(expert_kernel, kinds), grid_spec=pltpu.P...  35 us
    pallas_call x1, Pallas kernels, attend_back(): pl.pallas_call(functools.partial(attend_back_kernel, block, MAXLEN), grid...  23.2 us
    pallas_call x1, Pallas kernels, attend(): pl.pallas_call(functools.partial(attend_kernel, block, MAXLEN), grid_spec...  21 us
    ppermute x18, starting transfers between devices, flip(): return lax.ppermute(value, axis, [(i, i ^ bit) for i in range(size)])  16.9 us
  transfers between devices with their start and end apart: 68, of which 24 were waited for; matrix products, arithmetic and copies ran while one was open for 9% of the time, Pallas kernels for 21%

commit v1 on v0

--- a/solution.py
+++ b/solution.py
@@ -1190,14 +1190,14 @@
     )
     if many == 2:
         high_place = high
-        down_far = [swap(down_part[:2], "hi"), swap(down_part[2:], "hi")]
+        down_far = [swap(down_part[:1], "hi"), swap(down_part[1:], "hi")]
         gate_both = jnp.where(
             high == 0, jnp.stack([w_gate, gate_far], axis=1), jnp.stack([gate_far, w_gate], axis=1)
         )
     else:
         high_place = jnp.zeros_like(high)
         down_all = by_halves(lax.all_gather(down_part, "hi"))
-        down_part, down_far = down_all[0], [down_all[1, :2], down_all[1, 2:]]
+        down_part, down_far = down_all[0], [down_all[1, :1], down_all[1, 1:]]
         gate_both = lax.all_gather(w_gate, "hi", axis=1)
     out_pieces = [out_mine, swap(out_mine, "c"), out_other, swap(out_other, "c")]
 

time: 492 us -> 498 us (1.012)
    ppermute x36, waiting for transfers between devices: 86.1 us -> 97.7 us  [swap(): return lax.ppermute(value, axis, [(0, 1), (1, 0)])]
    ppermute x18, waiting for transfers between devices: 48.3 us -> 40.5 us  [flip(): return lax.ppermute(value, axis, [(i, i ^ bit) for i in range(size)])]
    ppermute x18, starting transfers between devices: 16.9 us -> 22.4 us  [flip(): return lax.ppermute(value, axis, [(i, i ^ bit) for i in range(size)])]
    unnamed x176 -> x174, local copies, waits for them, and re-layouts: 35.9 us -> 35.8 us
  transfers between devices with their start and end apart: 68 -> 68, of which waited for: 24 -> 25; matrix products, arithmetic and copies ran while one was open for 9% -> 9% of each run, Pallas kernels for 21% -> 21%
where the time goes in v1:
time: 498 us; the launch traced here: 489 us
  waiting for transfers between devices  153 us (31%)
  Pallas kernels  142 us (29%)
  starting transfers between devices  95.8 us (19%)
  local copies, waits for them, and re-layouts  53.4 us (11%)
  other arithmetic  29 us (6%)
  between operations  15.3 us (3%)
    ppermute x36, waiting for transfers between devices, swap(): return lax.ppermute(value, axis, [(0, 1), (1, 0)])  97.7 us
    ppermute x18, waiting for transfers between devices, flip(): return lax.ppermute(value, axis, [(i, i ^ bit) for i in range(size)])  40.5 us
    ppermute x36, starting transfers between devices, swap(): return lax.ppermute(value, axis, [(0, 1), (1, 0)])  36.9 us
    unnamed x174, local copies, waits for them, and re-layouts  35.8 us
    pallas_call x1, Pallas kernels, expert_pass(): pl.pallas_call(functools.partial(expert_kernel, kinds), grid_spec=pltpu.P...  35.1 us
    pallas_call x1, Pallas kernels, attend_back(): pl.pallas_call(functools.partial(attend_back_kernel, block, MAXLEN), grid...  23.2 us
    ppermute x18, starting transfers between devices, flip(): return lax.ppermute(value, axis, [(i, i ^ bit) for i in range(size)])  22.4 us
    pallas_call x1, Pallas kernels, attend(): pl.pallas_call(functools.partial(attend_kernel, block, MAXLEN), grid_spec...  21 us
  transfers between devices with their start and end apart: 68, of which 25 were waited for; matrix products, arithmetic and copies ran while one was open for 9% of the time, Pallas kernels for 21%

profile of v1, /device:TPU:1, one launch (start us, length us, event | category | flops | bytes accessed | tf_op | source)
XLA Modules:
  0.0 489.0 jit_solution(950006603151173271)
XLA Ops:
  9.8 3.1 collective-permute-start
  16.1 4.2 all-to-all-start
  31.0 10.0 %slots.1 = (s32[8,2048]{1,0:T(8,128)S(1)}, s32[2048,8]{1,0:T(8,128)S(1)}) custom-call(s32[8]{0:T(128)S(1)} %concatenate.22.scalars, s32[2048,2]{1,0:T(8,128)S(1)} %copy.52.routes_col.routes_ref, s32[2048,2]{1,0:T(8,128)S(1)} %copy.53.order_col, s32[2,2048]{1,0:T(2,128)S(1)} %bitcast.98, s32[2,2048]{1,0:T(2,128)S(1)} %bitcast.99), custom_call_target="tpu_custom_call" | custom-call | flops 9200000000 | bytes 65536 | tf_op jit(solution)/shard_map/slots/pallas_call | solution.py:776
  42.0 2.4 collective-permute-start.1
  45.6 7.3 %collective-permute-done.5.refs_7_ = bf16[2,96,768]{2,1,0:T(8,128)(2,1)} collective-permute-done((bf16[2,96,768]{2,1,0:T(8,128)(2,1)S(1)}, bf16[2,96,768]{2,1,0:T(8,128)(2,1)}, u32[]{:S(2)}, u32[]{:S(2)}) %collective-permute-start.5) | collective-permute-done | bytes 294944 | tf_op jit(solution)/shard_map/ppermute | solution.py:1049
  52.9 13.3 %collective-permute-done.6 = bf16[8,96,512]{2,1,0:T(8,128)(2,1)} collective-permute-done((bf16[8,96,512]{2,1,0:T(8,128)(2,1)}, bf16[8,96,512]{2,1,0:T(8,128)(2,1)}, u32[]{:S(2)}, u32[]{:S(2)}) %collective-permute-start.6) | collective-permute-done | bytes 786464 | tf_op jit(solution)/shard_map/ppermute | solution.py:29
  67.1 3.5 collective-permute-start.11
  73.7 4.2 all-to-all-start.1
  80.1 21.0 %attend.1 = (bf16[4,192,512]{2,1,0:T(8,128)(2,1)}, f32[3,1,2048]{2,1,0:T(1,128)S(1)}, bf16[576,2048]{1,0:T(8,128)(2,1)}, bf16[576,768]{1,0:T(8,128)(2,1)}) custom-call(s32[8]{0:T(128)S(1)} %concatenate.22.scalars, bf16[512,768]{1,0:T(8,128)(2,1)S(1)} %multiply_convert_fusion.1.refs_0_.refs_2_, bf16[512,768]{1,0:T(8,128)(2,1)S(1)} %collective-permute-done.1.refs_1_.refs_3_, ...), custom_call_target="tpu_custom_call" | custom-call | flops 27599998976 | bytes 65536 | tf_op jit(solution)/shard_map/attend/pallas_call | solution.py:152
  105.1 3.8 all-to-all-start.2
  108.9 3.3 maximum_select_fusion
  112.2 4.3 pick.2
  119.4 4.2 collective-permute-done.13.refs_3_
  123.6 4.4 all-to-all-start.3
  131.7 5.8 %middle.1 = (f32[512,768]{1,0:T(8,128)}, bf16[512,896]{1,0:T(8,128)(2,1)}, f32[512,128]{1,0:T(8,128)S(1)}) custom-call(s32[8]{0:T(128)S(1)} %concatenate.22.scalars, bf16[4,192,512]{2,1,0:T(8,128)(2,1)S(1)} %all-to-all-done.2.mixed, bf16[4,2,96,192]{3,2,1,0:T(8,128)(2,1)} %pad_maximum_fusion.1.p0, bf16[4,2,96,192]{3,2,1,0:T(8,128)(2,1)} %collective-permute-done.14.p1, ...), custom_call_target="tpu_custom_call" | custom-call | flops 6899999744 | bytes 65536 | tf_op jit(solution)/shard_map/middle/pallas_call | solution.py:831
  144.4 17.9 %collective-permute-done.20.refs_4_ = bf16[1,2,96,512]{3,2,1,0:T(8,128)(2,1)S(1)} collective-permute-done((bf16[1,2,96,512]{3,2,1,0:T(8,128)(2,1)S(1)}, bf16[1,2,96,512]{3,2,1,0:T(8,128)(2,1)S(1)}, u32[]{:S(2)}, u32[]{:S(2)}) %collective-permute-start.20) | collective-permute-done | bytes 196640 | tf_op jit(solution)/shard_map/ppermute | solution.py:29
  168.1 2.1 collective-permute-done.22.refs_3_
  170.2 4.9 %pick.3 = (bf16[192,896]{1,0:T(8,128)(2,1)S(1)}, bf16[192,896]{1,0:T(8,128)(2,1)S(1)}, bf16[192,896]{1,0:T(8,128)(2,1)S(1)}, bf16[192,896]{1,0:T(8,128)(2,1)S(1)}) custom-call(s32[8,2048]{1,0:T(8,128)S(1)} %get-tuple-element.175.ids_ref, bf16[512,896]{1,0:T(8,128)(2,1)} %get-tuple-element.188.refs_0_, bf16[512,896]{1,0:T(8,128)(2,1)} %collective-permute-done.21.refs_1_, ...), custom_call_target="tpu_custom_call" | custom-call | flops 5750000128 | bytes 65536 | tf_op jit(solution)/shard_map/pick/pallas_call | solution.py:588
  182.6 21.9 %collective-permute-done.33.refs_5_ = bf16[3,2,96,512]{3,2,1,0:T(8,128)(2,1)S(1)} collective-permute-done((bf16[3,2,96,512]{3,2,1,0:T(8,128)(2,1)S(1)}, bf16[3,2,96,512]{3,2,1,0:T(8,128)(2,1)S(1)}, u32[]{:S(2)}, u32[]{:S(2)}) %collective-permute-start.33) | collective-permute-done | bytes 589856 | tf_op jit(solution)/shard_map/ppermute | solution.py:29
  207.1 6.7 %collective-permute-done.25.refs_9_ = bf16[192,896]{1,0:T(8,128)(2,1)} collective-permute-done((bf16[192,896]{1,0:T(8,128)(2,1)S(1)}, bf16[192,896]{1,0:T(8,128)(2,1)}, u32[]{:S(2)}, u32[]{:S(2)}) %collective-permute-start.25) | collective-permute-done | bytes 344096 | tf_op jit(solution)/shard_map/ppermute | solution.py:1049
  213.8 2.2 collective-permute-start.27
  220.0 35.1 %expert_pass.1 = (f32[768,896]{1,0:T(8,128)}, bf16[768,896]{1,0:T(8,128)(2,1)}, f32[768,768]{1,0:T(8,128)}, bf16[768,768]{1,0:T(8,128)(2,1)}, bf16[2,4,2,3,96,512]{5,4,3,2,1,0:T(8,128)(2,1)}) custom-call(s32[2]{0:T(128)} %pad_add_fusion.scalars, bf16[4,2,2,96,512]{4,3,2,1,0:T(8,128)(2,1)} %bitcast.27.w_gate, bf16[4,2,96,512]{3,2,1,0:T(8,128)(2,1)} %bitcast.19.refs_0_, ...), custom_call_target="tpu_custom_call" | custom-call | flops 40249999360 | bytes 65536 | tf_op jit(solution)/shard_map/expert_pass/pallas_call | solution.py:522
  255.7 2.8 collective-permute-done.35.core_ref
  265.0 6.9 %collective-permute-done.36.refs_1_ = bf16[192,896]{1,0:T(8,128)(2,1)} collective-permute-done((bf16[192,896]{1,0:T(8,128)(2,1)}, bf16[192,896]{1,0:T(8,128)(2,1)}, u32[]{:S(2)}, u32[]{:S(2)}) %collective-permute-start.36) | collective-permute-done | bytes 344096 | tf_op jit(solution)/shard_map/ppermute | solution.py:1049
  272.2 11.9 %collective-permute-done.38.refs_3_ = bf16[192,896]{1,0:T(8,128)(2,1)} collective-permute-done((bf16[192,896]{1,0:T(8,128)(2,1)}, bf16[192,896]{1,0:T(8,128)(2,1)}, u32[]{:S(2)}, u32[]{:S(2)}) %collective-permute-start.38) | collective-permute-done | bytes 344096 | tf_op jit(solution)/shard_map/ppermute | solution.py:1049
  286.3 5.1 %spread.2 = (f32[2,512,896]{2,1,0:T(8,128)S(1)}, bf16[2,512,896]{2,1,0:T(8,128)(2,1)S(1)}) custom-call(s32[2048,8]{1,0:T(8,128)S(1)} %copy-done.49, bf16[192,896]{1,0:T(8,128)(2,1)S(1)} %copy-done.45, bf16[192,896]{1,0:T(8,128)(2,1)} %collective-permute-done.36.refs_1_, bf16[192,896]{1,0:T(8,128)(2,1)} %collective-permute-done.37.refs_2_, ...), custom_call_target="tpu_custom_call" | custom-call | flops 34500001792 | bytes 65536 | tf_op jit(solution)/shard_map/spread/pallas_call | solution.py:693
  291.5 3.1 collective-permute-start.40
  294.6 3.4 collective-permute-done.40.got_ref
  307.6 13.9 %collective-permute-done.41.far_ref = bf16[512,896]{1,0:T(8,128)(2,1)S(1)} collective-permute-done((bf16[512,896]{1,0:T(8,128)(2,1)}, bf16[512,896]{1,0:T(8,128)(2,1)S(1)}, u32[]{:S(2)}, u32[]{:S(2)}) %collective-permute-start.41) | collective-permute-done | bytes 917536 | tf_op jit(solution)/shard_map/ppermute | solution.py:29
  323.6 8.9 %router_back.1 = (f32[512,768]{1,0:T(8,128)}, bf16[512,768]{1,0:T(8,128)(2,1)S(1)}, f32[512,768]{1,0:T(8,128)}, f32[512,12]{1,0:T(8,128)S(1)}, f32[32,768]{1,0:T(8,128)S(1)}) custom-call(s32[8]{0:T(128)S(1)} %concatenate.22.scalars, f32[2,512,896]{2,1,0:T(8,128)} %copy-done.1, bf16[2,512,896]{2,1,0:T(8,128)(2,1)} %copy-done.58, ...), custom_call_target="tpu_custom_call" | custom-call | flops 9200000000 | bytes 65536 | tf_op jit(solution)/shard_map/router_back/pallas_call | solution.py:996
  332.5 3.1 mixed_back.1
  339.8 2.6 collective-permute-start.46
  343.2 5.0 %all-to-all-start.4 = ((f32[32,1,768]{2,1,0:T(1,128)}), f32[32,1,768]{2,1,0:T(1,128)}, u32[]{:S(2)}, u32[]{:S(2)}) async-start(f32[32,1,768]{2,1,0:T(1,128)} %copy.58), calls=%async_computation.5 | async-start | bytes 196608 | tf_op jit(solution)/shard_map/all_to_all | solution.py:1260
  348.1 2.4 collective-permute-start.47
  358.4 23.2 %attend_back.1 = bf16[4,3,192,512]{3,2,1,0:T(8,128)(2,1)S(1)} custom-call(s32[8]{0:T(128)S(1)} %concatenate.22.scalars, bf16[576,2048]{1,0:T(8,128)(2,1)S(1)} %copy-done.55, f32[3,1,2048]{2,1,0:T(1,128)S(1)} %get-tuple-element.252.lse_ref, bf16[192,512]{1,0:T(8,128)(2,1)S(1)} %copy-done.52, bf16[192,512]{1,0:T(8,128)(2,1)S(1)} %collective-permute-done.42.refs_1_, ...), custom_call_target="tpu_custom_call" | custom-call | flops 39099998208 | bytes 65536 | tf_op jit(solution)/shard_map/attend_back/pallas_call | solution.py:294
  381.7 4.3 collective-permute-done.47.refs_3_
  391.5 4.9 %spread.3 = (f32[2,512,768]{2,1,0:T(8,128)S(1)}, bf16[2,512,768]{2,1,0:T(8,128)(2,1)}) custom-call(s32[2048,8]{1,0:T(8,128)S(1)} %copy-done.50, bf16[192,768]{1,0:T(8,128)(2,1)S(1)} %copy-done.47, bf16[192,768]{1,0:T(8,128)(2,1)S(1)} %copy-done.28, bf16[192,768]{1,0:T(8,128)(2,1)} %collective-permute-done.46.refs_2_, bf16[192,768]{1,0:T(8,128)(2,1)S(1)} %copy-done.36), custom_call_target="tpu_custom_call" | custom-call | flops 34500001792 | bytes 65536 | tf_op jit(solution)/shard_map/spread/pallas_call | solution.py:693
  396.8 4.4 all-to-all-start.5
  404.6 6.9 %attn_grads.1 = (bf16[4,96,768]{2,1,0:T(8,128)(2,1)S(1)}, bf16[4,96,768]{2,1,0:T(8,128)(2,1)}) custom-call(s32[8]{0:T(128)S(1)} %concatenate.22.scalars, bf16[4,576,512]{2,1,0:T(8,128)(2,1)} %bitcast.96, bf16[4,192,512]{2,1,0:T(8,128)(2,1)} %get-tuple-element.174.refs_1_, bf16[512,768]{1,0:T(8,128)(2,1)S(1)} %copy-done.3, bf16[512,768]{1,0:T(8,128)(2,1)S(1)} %copy-done.21, ...), custom_call_target="tpu_custom_call" | custom-call | flops 34500001792 | bytes 65536 | tf_op jit(solution)/shard_map/attn_grads/pallas_call | solution.py:208
  414.8 2.2 fusion.3
  417.0 13.1 %collective-permute-done.51.g3 = bf16[576,512]{1,0:T(8,128)(2,1)} collective-permute-done((bf16[576,512]{1,0:T(8,128)(2,1)}, bf16[576,512]{1,0:T(8,128)(2,1)}, u32[]{:S(2)}, u32[]{:S(2)}) %collective-permute-start.51) | collective-permute-done | bytes 589856 | tf_op jit(solution)/shard_map/ppermute | solution.py:606
  430.2 13.6 %collective-permute-done.54 = bf16[4,96,768]{2,1,0:T(8,128)(2,1)} collective-permute-done((bf16[4,96,768]{2,1,0:T(8,128)(2,1)}, bf16[4,96,768]{2,1,0:T(8,128)(2,1)}, u32[]{:S(2)}, u32[]{:S(2)}) %collective-permute-start.54) | collective-permute-done | bytes 589856 | tf_op jit(solution)/shard_map/ppermute | solution.py:29
  443.8 2.3 fusion.9
  446.9 4.7 collective-permute-start.59
  451.8 6.7 %inputs_back.1 = (f32[512,768]{1,0:T(8,128)}, f32[2,1,768]{2,1,0:T(1,128)S(1)}) custom-call(bf16[576,512]{1,0:T(8,128)(2,1)S(1)} %copy-done.5, bf16[576,512]{1,0:T(8,128)(2,1)} %collective-permute-done.49.g1, bf16[576,512]{1,0:T(8,128)(2,1)} %collective-permute-done.50.g2, bf16[576,512]{1,0:T(8,128)(2,1)} %collective-permute-done.51.g3, ...), custom_call_target="tpu_custom_call" | custom-call | flops 6899999744 | bytes 65536 | tf_op jit(solution)/shard_map/inputs_back/pallas_call | solution.py:376
  461.2 5.1 %all-to-all-start.6 = ((f32[32,1,1536]{2,1,0:T(1,128)}), f32[32,1,1536]{2,1,0:T(1,128)}, u32[]{:S(2)}, u32[]{:S(2)}) async-start(f32[32,1,1536]{2,1,0:T(1,128)} %broadcast_in_dim.5), calls=%async_computation.7 | async-start | bytes 393216 | tf_op jit(solution)/shard_map/all_to_all | solution.py:1045
  466.3 3.3 fusion.1
  469.6 4.0 convert_bitcast_fusion
  (331 shorter events, 120.2 us)
Async XLA Ops:
  9.8 17.4 %collective-permute-start = (bf16[96,768]{1,0:T(8,128)(2,1)}, bf16[96,768]{1,0:T(8,128)(2,1)}, u32[]{:S(2)}, u32[]{:S(2)}) collective-permute-start(bf16[96,768]{1,0:T(8,128)(2,1)} %pad_maximum_fusion.3), channel_id=1, source_target_pairs={{0,16},{16,0},{1,17},{17,1},{2,18},{18,2},{3,19},{19,3},{4,20},{20... | collective-permute-start | bytes 442376 | tf_op jit(solution)/shard_map/ppermute | solution.py:29
  14.8 38.0 %collective-permute-start.2 = (bf16[512,768]{1,0:T(8,128)(2,1)S(1)}, bf16[512,768]{1,0:T(8,128)(2,1)}, u32[]{:S(2)}, u32[]{:S(2)}) collective-permute-start(bf16[512,768]{1,0:T(8,128)(2,1)S(1)} %multiply_convert_fusion.1.refs_0_.refs_2_), channel_id=1, source_target_pairs={{0,2},{2,0},{1,3},{3,1},{4,6},{6,4},{5,7},{7,5},{8,10},{10,8},{9,1... | collective-permute-start | bytes 2359304 | tf_op jit(solution)/shard_map/ppermute | solution.py:29
  16.1 50.0 %all-to-all-start = ((bf16[8,96,512]{2,1,0:T(8,128)(2,1)}), bf16[8,96,512]{2,1,0:T(8,128)(2,1)}, u32[]{:S(2)}, u32[]{:S(2)}) async-start(bf16[8,96,512]{2,1,0:T(8,128)(2,1)} %param.36), calls=%async_computation | async-start | bytes 1572864 | tf_op jit(solution)/shard_map/all_to_all | solution.py:1147
  28.3 13.7 %collective-permute-start.3 = (bf16[2,96,768]{2,1,0:T(8,128)(2,1)S(1)}, bf16[2,96,768]{2,1,0:T(8,128)(2,1)}, u32[]{:S(2)}, u32[]{:S(2)}) collective-permute-start(bf16[2,96,768]{2,1,0:T(8,128)(2,1)S(1)} %pad_maximum_fusion.2.refs_4_), channel_id=1, source_target_pairs={{0,4},{4,0},{8,12},{12,8},{1,5},{5,1},{9,13},{13,9},{2,6},{6,2},{1... | collective-permute-start | bytes 884744 | tf_op jit(solution)/shard_map/ppermute | solution.py:1049
  29.7 15.9 %collective-permute-start.4 = (bf16[2,96,768]{2,1,0:T(8,128)(2,1)S(1)}, bf16[2,96,768]{2,1,0:T(8,128)(2,1)}, u32[]{:S(2)}, u32[]{:S(2)}) collective-permute-start(bf16[2,96,768]{2,1,0:T(8,128)(2,1)S(1)} %pad_maximum_fusion.2.refs_4_), channel_id=1, source_target_pairs={{0,8},{4,12},{8,0},{12,4},{1,9},{5,13},{9,1},{13,5},{2,10},{6,14},... | collective-permute-start | bytes 884744 | tf_op jit(solution)/shard_map/ppermute | solution.py:1049
  30.9 22.0 %collective-permute-start.5 = (bf16[2,96,768]{2,1,0:T(8,128)(2,1)S(1)}, bf16[2,96,768]{2,1,0:T(8,128)(2,1)}, u32[]{:S(2)}, u32[]{:S(2)}) collective-permute-start(bf16[2,96,768]{2,1,0:T(8,128)(2,1)S(1)} %pad_maximum_fusion.2.refs_4_), channel_id=1, source_target_pairs={{0,12},{4,8},{8,4},{12,0},{1,13},{5,9},{9,5},{13,1},{2,14},{6,10},... | collective-permute-start | bytes 884744 | tf_op jit(solution)/shard_map/ppermute | solution.py:1049
  31.0 35.1 %collective-permute-start.6 = (bf16[8,96,512]{2,1,0:T(8,128)(2,1)}, bf16[8,96,512]{2,1,0:T(8,128)(2,1)}, u32[]{:S(2)}, u32[]{:S(2)}) collective-permute-start(bf16[8,96,512]{2,1,0:T(8,128)(2,1)} %param.35), channel_id=1, source_target_pairs={{0,16},{16,0},{1,17},{17,1},{2,18},{18,2},{3,19},{19,3},{4,20},{20... | collective-permute-start | bytes 2359304 | tf_op jit(solution)/shard_map/ppermute | solution.py:29
  42.0 37.9 %collective-permute-start.1 = (bf16[512,768]{1,0:T(8,128)(2,1)S(1)}, bf16[512,768]{1,0:T(8,128)(2,1)S(1)}, u32[]{:S(2)}, u32[]{:S(2)}) collective-permute-start(bf16[512,768]{1,0:T(8,128)(2,1)S(1)} %multiply_convert_fusion.1.refs_0_.refs_2_), channel_id=1, source_target_pairs={{0,1},{1,0},{2,3},{3,2},{4,5},{5,4},{6,7},{7,6},{8,9},{9,8},{10,11... | collective-permute-start | bytes 2359304 | tf_op jit(solution)/shard_map/ppermute | solution.py:29
  66.1 35.8 %collective-permute-start.10 = (bf16[512,768]{1,0:T(8,128)(2,1)}, bf16[512,768]{1,0:T(8,128)(2,1)}, u32[]{:S(2)}, u32[]{:S(2)}) collective-permute-start(bf16[512,768]{1,0:T(8,128)(2,1)} %multiply_convert_fusion.refs_0_), channel_id=1, source_target_pairs={{0,2},{2,0},{1,3},{3,1},{4,6},{6,4},{5,7},{7,5},{8,10},{10,8},{9,1... | collective-permute-start | bytes 2359304 | tf_op jit(solution)/shard_map/ppermute | solution.py:29
  67.1 45.1 %collective-permute-start.11 = (bf16[512,768]{1,0:T(8,128)(2,1)}, bf16[512,768]{1,0:T(8,128)(2,1)}, u32[]{:S(2)}, u32[]{:S(2)}) collective-permute-start(bf16[512,768]{1,0:T(8,128)(2,1)} %multiply_convert_fusion.refs_0_), channel_id=1, source_target_pairs={{0,1},{1,0},{2,3},{3,2},{4,5},{5,4},{6,7},{7,6},{8,9},{9,8},{10,11... | collective-permute-start | bytes 2359304 | tf_op jit(solution)/shard_map/ppermute | solution.py:29
  73.6 27.5 %collective-permute-start.8 = (bf16[4,2,96,192]{3,2,1,0:T(8,128)(2,1)}, bf16[4,2,96,192]{3,2,1,0:T(8,128)(2,1)}, u32[]{:S(2)}, u32[]{:S(2)}) collective-permute-start(bf16[4,2,96,192]{3,2,1,0:T(8,128)(2,1)} %pad_maximum_fusion.1.p0), channel_id=1, source_target_pairs={{0,2},{2,0},{1,3},{3,1},{4,6},{6,4},{5,7},{7,5},{8,10},{10,8},{9,1... | collective-permute-start | bytes 884744 | tf_op jit(solution)/shard_map/ppermute | solution.py:29
  73.7 28.2 %all-to-all-start.1 = ((bf16[8,96,512]{2,1,0:T(8,128)(2,1)}), bf16[8,96,512]{2,1,0:T(8,128)(2,1)}, u32[]{:S(2)}, u32[]{:S(2)}) async-start(bf16[8,96,512]{2,1,0:T(8,128)(2,1)} %bitcast.101), calls=%async_computation.1 | async-start | bytes 1572864 | tf_op jit(solution)/shard_map/all_to_all | solution.py:1177
  79.9 21.3 %collective-permute-start.9 = (bf16[2,2,96,512]{3,2,1,0:T(8,128)(2,1)S(1)}, bf16[2,2,96,512]{3,2,1,0:T(8,128)(2,1)S(1)}, u32[]{:S(2)}, u32[]{:S(2)}) collective-permute-start(bf16[2,2,96,512]{3,2,1,0:T(8,128)(2,1)S(1)} %get-tuple-element.344), channel_id=1, source_target_pairs={{0,16},{16,0},{1,17},{17,1},{2,18},{18,2},{3,19},{19,3},{4,20},{20... | collective-permute-start | bytes 1179656 | tf_op jit(solution)/shard_map/ppermute | solution.py:29
  103.2 20.3 %collective-permute-start.13 = (bf16[2,2,96,512]{3,2,1,0:T(8,128)(2,1)}, bf16[2,2,96,512]{3,2,1,0:T(8,128)(2,1)}, u32[]{:S(2)}, u32[]{:S(2)}) collective-permute-start(bf16[2,2,96,512]{3,2,1,0:T(8,128)(2,1)} %get-tuple-element.343), channel_id=1, source_target_pairs={{0,16},{16,0},{1,17},{17,1},{2,18},{18,2},{3,19},{19,3},{4,20},{20... | collective-permute-start | bytes 1179656 | tf_op jit(solution)/shard_map/ppermute | solution.py:29
  105.1 18.5 %all-to-all-start.2 = ((bf16[4,192,512]{2,1,0:T(8,128)(2,1)}), bf16[4,192,512]{2,1,0:T(8,128)(2,1)S(1)}, u32[]{:S(2)}, u32[]{:S(2)}) async-start(bf16[4,192,512]{2,1,0:T(8,128)(2,1)} %get-tuple-element.174.refs_1_), calls=%async_computation.2 | async-start | bytes 1572864 | tf_op jit(solution)/shard_map/all_to_all | solution.py:1204
  123.6 43.7 %all-to-all-start.3 = ((bf16[8,2,96,512]{3,2,1,0:T(8,128)(2,1)}), bf16[8,2,96,512]{3,2,1,0:T(8,128)(2,1)}, u32[]{:S(2)}, u32[]{:S(2)}) async-start(bf16[8,2,96,512]{3,2,1,0:T(8,128)(2,1)} %maximum_select_fusion), calls=%async_computation.3 | async-start | bytes 3145728 | tf_op jit(solution)/shard_map/all_to_all | solution.py:1217
  128.0 258.7 %reduce-scatter.2.cloned.1.call-start = ((), (), s32[]{:S(2)}) async-start(), calls=%async_computation.8 | async-start | bytes 7077888 | tf_op jit(solution)/shard_map/reduce_scatter | solution.py:1071
  137.5 29.7 %collective-permute-start.16 = (bf16[512,896]{1,0:T(8,128)(2,1)}, bf16[512,896]{1,0:T(8,128)(2,1)S(1)}, u32[]{:S(2)}, u32[]{:S(2)}) collective-permute-start(bf16[512,896]{1,0:T(8,128)(2,1)} %get-tuple-element.188.refs_0_), channel_id=1, source_target_pairs={{0,2},{2,0},{1,3},{3,1},{4,6},{6,4},{5,7},{7,5},{8,10},{10,8},{9,1... | collective-permute-start | bytes 2752520 | tf_op jit(solution)/shard_map/ppermute | solution.py:29
  139.2 24.6 %collective-permute-start.17 = (bf16[192,768]{1,0:T(8,128)(2,1)S(1)}, bf16[192,768]{1,0:T(8,128)(2,1)S(1)}, u32[]{:S(2)}, u32[]{:S(2)}) collective-permute-start(bf16[192,768]{1,0:T(8,128)(2,1)S(1)} %copy-done.34), channel_id=1, source_target_pairs={{0,4},{4,0},{8,12},{12,8},{1,5},{5,1},{9,13},{13,9},{2,6},{6,2},{1... | collective-permute-start | bytes 884744 | tf_op jit(solution)/shard_map/ppermute | solution.py:1049
  140.3 23.5 %collective-permute-start.18 = (bf16[192,768]{1,0:T(8,128)(2,1)S(1)}, bf16[192,768]{1,0:T(8,128)(2,1)S(1)}, u32[]{:S(2)}, u32[]{:S(2)}) collective-permute-start(bf16[192,768]{1,0:T(8,128)(2,1)S(1)} %copy-done.32), channel_id=1, source_target_pairs={{0,8},{4,12},{8,0},{12,4},{1,9},{5,13},{9,1},{13,5},{2,10},{6,14},... | collective-permute-start | bytes 884744 | tf_op jit(solution)/shard_map/ppermute | solution.py:1049
  141.5 23.5 %collective-permute-start.19 = (bf16[192,768]{1,0:T(8,128)(2,1)S(1)}, bf16[192,768]{1,0:T(8,128)(2,1)S(1)}, u32[]{:S(2)}, u32[]{:S(2)}) collective-permute-start(bf16[192,768]{1,0:T(8,128)(2,1)S(1)} %copy-done.30), channel_id=1, source_target_pairs={{0,12},{4,8},{8,4},{12,0},{1,13},{5,9},{9,5},{13,1},{2,14},{6,10},... | collective-permute-start | bytes 884744 | tf_op jit(solution)/shard_map/ppermute | solution.py:1049
  142.8 19.6 %collective-permute-start.20 = (bf16[1,2,96,512]{3,2,1,0:T(8,128)(2,1)S(1)}, bf16[1,2,96,512]{3,2,1,0:T(8,128)(2,1)S(1)}, u32[]{:S(2)}, u32[]{:S(2)}) collective-permute-start(bf16[1,2,96,512]{3,2,1,0:T(8,128)(2,1)S(1)} %slice.133), channel_id=1, source_target_pairs={{0,16},{16,0},{1,17},{17,1},{2,18},{18,2},{3,19},{19,3},{4,20},{20... | collective-permute-start | bytes 589832 | tf_op jit(solution)/shard_map/ppermute | solution.py:29
  175.2 31.4 %collective-permute-start.31 = (bf16[576,768]{1,0:T(8,128)(2,1)}, bf16[576,768]{1,0:T(8,128)(2,1)S(1)}, u32[]{:S(2)}, u32[]{:S(2)}) collective-permute-start(bf16[576,768]{1,0:T(8,128)(2,1)} %get-tuple-element.286.p0), channel_id=1, source_target_pairs={{0,2},{2,0},{1,3},{3,1},{4,6},{6,4},{5,7},{7,5},{8,10},{10,8},{9,1... | collective-permute-start | bytes 2654216 | tf_op jit(solution)/shard_map/ppermute | solution.py:29
  176.4 28.1 %collective-permute-start.33 = (bf16[3,2,96,512]{3,2,1,0:T(8,128)(2,1)S(1)}, bf16[3,2,96,512]{3,2,1,0:T(8,128)(2,1)S(1)}, u32[]{:S(2)}, u32[]{:S(2)}) collective-permute-start(bf16[3,2,96,512]{3,2,1,0:T(8,128)(2,1)S(1)} %slice.134), channel_id=1, source_target_pairs={{0,16},{16,0},{1,17},{17,1},{2,18},{18,2},{3,19},{19,3},{4,20},{20... | collective-permute-start | bytes 1769480 | tf_op jit(solution)/shard_map/ppermute | solution.py:29
  178.0 27.8 %collective-permute-start.23 = (bf16[192,896]{1,0:T(8,128)(2,1)S(1)}, bf16[192,896]{1,0:T(8,128)(2,1)S(1)}, u32[]{:S(2)}, u32[]{:S(2)}) collective-permute-start(bf16[192,896]{1,0:T(8,128)(2,1)S(1)} %get-tuple-element.206), channel_id=1, source_target_pairs={{0,4},{4,0},{8,12},{12,8},{1,5},{5,1},{9,13},{13,9},{2,6},{6,2},{1... | collective-permute-start | bytes 1032200 | tf_op jit(solution)/shard_map/ppermute | solution.py:1049
  180.3 39.7 %collective-permute-start.34 = (bf16[768,768]{1,0:T(8,128)(2,1)}, bf16[768,768]{1,0:T(8,128)(2,1)}, u32[]{:S(2)}, u32[]{:S(2)}) collective-permute-start(bf16[768,768]{1,0:T(8,128)(2,1)} %pad_maximum_fusion), channel_id=1, source_target_pairs={{0,1},{1,0},{2,3},{3,2},{4,5},{5,4},{6,7},{7,6},{8,9},{9,8},{10,11... | collective-permute-start | bytes 3538952 | tf_op jit(solution)/shard_map/ppermute | solution.py:29
  181.4 25.2 %collective-permute-start.24 = (bf16[192,896]{1,0:T(8,128)(2,1)S(1)}, bf16[192,896]{1,0:T(8,128)(2,1)}, u32[]{:S(2)}, u32[]{:S(2)}) collective-permute-start(bf16[192,896]{1,0:T(8,128)(2,1)S(1)} %get-tuple-element.207), channel_id=1, source_target_pairs={{0,8},{4,12},{8,0},{12,4},{1,9},{5,13},{9,1},{13,5},{2,10},{6,14},... | collective-permute-start | bytes 1032200 | tf_op jit(solution)/shard_map/ppermute | solution.py:1049
  205.8 14.2 %collective-permute-start.30 = (bf16[576,768]{1,0:T(8,128)(2,1)}, bf16[576,768]{1,0:T(8,128)(2,1)}, u32[]{:S(2)}, u32[]{:S(2)}) collective-permute-start(bf16[576,768]{1,0:T(8,128)(2,1)} %get-tuple-element.286.p0), channel_id=1, source_target_pairs={{0,1},{1,0},{2,3},{3,2},{4,5},{5,4},{6,7},{7,6},{8,9},{9,8},{10,11... | collective-permute-start | bytes 2654216 | tf_op jit(solution)/shard_map/ppermute | solution.py:29
  206.6 13.5 %collective-permute-start.32 = (bf16[576,768]{1,0:T(8,128)(2,1)S(1)}, bf16[576,768]{1,0:T(8,128)(2,1)}, u32[]{:S(2)}, u32[]{:S(2)}) collective-permute-start(bf16[576,768]{1,0:T(8,128)(2,1)S(1)} %collective-permute-done.31.p2), channel_id=1, source_target_pairs={{0,1},{1,0},{2,3},{3,2},{4,5},{5,4},{6,7},{7,6},{8,9},{9,8},{10,11... | collective-permute-start | bytes 2654216 | tf_op jit(solution)/shard_map/ppermute | solution.py:29
  263.9 20.3 %collective-permute-start.38 = (bf16[192,896]{1,0:T(8,128)(2,1)}, bf16[192,896]{1,0:T(8,128)(2,1)}, u32[]{:S(2)}, u32[]{:S(2)}) collective-permute-start(bf16[192,896]{1,0:T(8,128)(2,1)} %get-tuple-element.228), channel_id=1, source_target_pairs={{0,12},{4,8},{8,4},{12,0},{1,13},{5,9},{9,5},{13,1},{2,14},{6,10},... | collective-permute-start | bytes 1032200 | tf_op jit(solution)/shard_map/ppermute | solution.py:1049
  299.6 21.9 %collective-permute-start.41 = (bf16[512,896]{1,0:T(8,128)(2,1)}, bf16[512,896]{1,0:T(8,128)(2,1)S(1)}, u32[]{:S(2)}, u32[]{:S(2)}) collective-permute-start(bf16[512,896]{1,0:T(8,128)(2,1)} %fusion.2), channel_id=1, source_target_pairs={{0,2},{2,0},{1,3},{3,1},{4,6},{6,4},{5,7},{7,5},{8,10},{10,8},{9,1... | collective-permute-start | bytes 2752520 | tf_op jit(solution)/shard_map/ppermute | solution.py:29
  336.3 11.9 %collective-permute-start.42 = (bf16[192,512]{1,0:T(8,128)(2,1)S(1)}, bf16[192,512]{1,0:T(8,128)(2,1)S(1)}, u32[]{:S(2)}, u32[]{:S(2)}) collective-permute-start(bf16[192,512]{1,0:T(8,128)(2,1)S(1)} %get-tuple-element.255), channel_id=1, source_target_pairs={{0,1},{1,0},{2,3},{3,2},{4,5},{5,4},{6,7},{7,6},{8,9},{9,8},{10,11... | collective-permute-start | bytes 589832 | tf_op jit(solution)/shard_map/ppermute | solution.py:606
  337.4 13.1 %collective-permute-start.43 = (bf16[192,512]{1,0:T(8,128)(2,1)S(1)}, bf16[192,512]{1,0:T(8,128)(2,1)S(1)}, u32[]{:S(2)}, u32[]{:S(2)}) collective-permute-start(bf16[192,512]{1,0:T(8,128)(2,1)S(1)} %get-tuple-element.256), channel_id=1, source_target_pairs={{0,2},{1,3},{2,0},{3,1},{4,6},{5,7},{6,4},{7,5},{8,10},{9,11},{10,... | collective-permute-start | bytes 589832 | tf_op jit(solution)/shard_map/ppermute | solution.py:606
  339.0 12.2 %collective-permute-start.44 = (bf16[192,512]{1,0:T(8,128)(2,1)S(1)}, bf16[192,512]{1,0:T(8,128)(2,1)S(1)}, u32[]{:S(2)}, u32[]{:S(2)}) collective-permute-start(bf16[192,512]{1,0:T(8,128)(2,1)S(1)} %get-tuple-element.257), channel_id=1, source_target_pairs={{0,3},{1,2},{2,1},{3,0},{4,7},{5,6},{6,5},{7,4},{8,11},{9,10},{10,... | collective-permute-start | bytes 589832 | tf_op jit(solution)/shard_map/ppermute | solution.py:606
  339.0 42.6 %collective-permute-start.45 = (bf16[192,768]{1,0:T(8,128)(2,1)}, bf16[192,768]{1,0:T(8,128)(2,1)S(1)}, u32[]{:S(2)}, u32[]{:S(2)}) collective-permute-start(bf16[192,768]{1,0:T(8,128)(2,1)} %get-tuple-element.263), channel_id=1, source_target_pairs={{0,4},{4,0},{8,12},{12,8},{1,5},{5,1},{9,13},{13,9},{2,6},{6,2},{1... | collective-permute-start | bytes 884744 | tf_op jit(solution)/shard_map/ppermute | solution.py:1049
  339.8 41.9 %collective-permute-start.46 = (bf16[192,768]{1,0:T(8,128)(2,1)}, bf16[192,768]{1,0:T(8,128)(2,1)}, u32[]{:S(2)}, u32[]{:S(2)}) collective-permute-start(bf16[192,768]{1,0:T(8,128)(2,1)} %get-tuple-element.264), channel_id=1, source_target_pairs={{0,8},{4,12},{8,0},{12,4},{1,9},{5,13},{9,1},{13,5},{2,10},{6,14},... | collective-permute-start | bytes 884744 | tf_op jit(solution)/shard_map/ppermute | solution.py:1049
  343.2 53.6 %all-to-all-start.4 = ((f32[32,1,768]{2,1,0:T(1,128)}), f32[32,1,768]{2,1,0:T(1,128)}, u32[]{:S(2)}, u32[]{:S(2)}) async-start(f32[32,1,768]{2,1,0:T(1,128)} %copy.58), calls=%async_computation.5 | async-start | bytes 196608 | tf_op jit(solution)/shard_map/all_to_all | solution.py:1260
  348.1 37.8 %collective-permute-start.47 = (bf16[192,768]{1,0:T(8,128)(2,1)S(1)}, bf16[192,768]{1,0:T(8,128)(2,1)S(1)}, u32[]{:S(2)}, u32[]{:S(2)}) collective-permute-start(bf16[192,768]{1,0:T(8,128)(2,1)S(1)} %copy-done.26), channel_id=1, source_target_pairs={{0,12},{4,8},{8,4},{12,0},{1,13},{5,9},{9,5},{13,1},{2,14},{6,10},... | collective-permute-start | bytes 884744 | tf_op jit(solution)/shard_map/ppermute | solution.py:1049
  351.9 34.9 %collective-permute-start.48 = (bf16[512,768]{1,0:T(8,128)(2,1)}, bf16[512,768]{1,0:T(8,128)(2,1)}, u32[]{:S(2)}, u32[]{:S(2)}) collective-permute-start(bf16[512,768]{1,0:T(8,128)(2,1)} %copy-done.22), channel_id=1, source_target_pairs={{0,2},{2,0},{1,3},{3,1},{4,6},{6,4},{5,7},{7,5},{8,10},{10,8},{9,1... | collective-permute-start | bytes 2359304 | tf_op jit(solution)/shard_map/ppermute | solution.py:29
  353.1 43.4 %collective-permute-start.52 = (bf16[512,768]{1,0:T(8,128)(2,1)}, bf16[512,768]{1,0:T(8,128)(2,1)}, u32[]{:S(2)}, u32[]{:S(2)}) collective-permute-start(bf16[512,768]{1,0:T(8,128)(2,1)} %copy-done.22), channel_id=1, source_target_pairs={{0,1},{1,0},{2,3},{3,2},{4,5},{5,4},{6,7},{7,6},{8,9},{9,8},{10,11... | collective-permute-start | bytes 2359304 | tf_op jit(solution)/shard_map/ppermute | solution.py:29
  388.2 28.8 %collective-permute-start.49 = (bf16[576,512]{1,0:T(8,128)(2,1)}, bf16[576,512]{1,0:T(8,128)(2,1)}, u32[]{:S(2)}, u32[]{:S(2)}) collective-permute-start(bf16[576,512]{1,0:T(8,128)(2,1)} %get-tuple-element.339), channel_id=1, source_target_pairs={{0,1},{1,0},{2,3},{3,2},{4,5},{5,4},{6,7},{7,6},{8,9},{9,8},{10,11... | collective-permute-start | bytes 1769480 | tf_op jit(solution)/shard_map/ppermute | solution.py:606
  388.7 28.4 %collective-permute-start.50 = (bf16[576,512]{1,0:T(8,128)(2,1)}, bf16[576,512]{1,0:T(8,128)(2,1)}, u32[]{:S(2)}, u32[]{:S(2)}) collective-permute-start(bf16[576,512]{1,0:T(8,128)(2,1)} %get-tuple-element.338), channel_id=1, source_target_pairs={{0,2},{1,3},{2,0},{3,1},{4,6},{5,7},{6,4},{7,5},{8,10},{9,11},{10,... | collective-permute-start | bytes 1769480 | tf_op jit(solution)/shard_map/ppermute | solution.py:606
  389.8 40.3 %collective-permute-start.51 = (bf16[576,512]{1,0:T(8,128)(2,1)}, bf16[576,512]{1,0:T(8,128)(2,1)}, u32[]{:S(2)}, u32[]{:S(2)}) collective-permute-start(bf16[576,512]{1,0:T(8,128)(2,1)} %get-tuple-element.337), channel_id=1, source_target_pairs={{0,3},{1,2},{2,1},{3,0},{4,7},{5,6},{6,5},{7,4},{8,11},{9,10},{10,... | collective-permute-start | bytes 1769480 | tf_op jit(solution)/shard_map/ppermute | solution.py:606
  396.4 18.3 %collective-permute-start.55 = (bf16[2,512,768]{2,1,0:T(8,128)(2,1)}, bf16[2,512,768]{2,1,0:T(8,128)(2,1)}, u32[]{:S(2)}, u32[]{:S(2)}) collective-permute-start(bf16[2,512,768]{2,1,0:T(8,128)(2,1)} %get-tuple-element.278), channel_id=1, source_target_pairs={{0,1},{1,0},{2,3},{3,2},{4,5},{5,4},{6,7},{7,6},{8,9},{9,8},{10,11... | collective-permute-start | bytes 4718600 | tf_op jit(solution)/shard_map/ppermute | solution.py:29
  396.8 63.6 %all-to-all-start.5 = ((bf16[8,3,96,512]{3,2,1,0:T(8,128)(2,1)}), bf16[8,3,96,512]{3,2,1,0:T(8,128)(2,1)}, u32[]{:S(2)}, u32[]{:S(2)}) async-start(bf16[8,3,96,512]{3,2,1,0:T(8,128)(2,1)} %bitcast.100), calls=%async_computation.6 | async-start | bytes 4718592 | tf_op jit(solution)/shard_map/all_to_all | solution.py:1269
  412.3 31.5 %collective-permute-start.54 = (bf16[4,96,768]{2,1,0:T(8,128)(2,1)}, bf16[4,96,768]{2,1,0:T(8,128)(2,1)}, u32[]{:S(2)}, u32[]{:S(2)}) collective-permute-start(bf16[4,96,768]{2,1,0:T(8,128)(2,1)} %get-tuple-element.272), channel_id=1, source_target_pairs={{0,16},{16,0},{1,17},{17,1},{2,18},{18,2},{3,19},{19,3},{4,20},{20... | collective-permute-start | bytes 1769480 | tf_op jit(solution)/shard_map/ppermute | solution.py:29
  443.8 22.5 %collective-permute-start.56 = (bf16[512,768]{1,0:T(8,128)(2,1)}, bf16[512,768]{1,0:T(8,128)(2,1)}, u32[]{:S(2)}, u32[]{:S(2)}) collective-permute-start(bf16[512,768]{1,0:T(8,128)(2,1)} %fusion.3), channel_id=1, source_target_pairs={{0,2},{2,0},{1,3},{3,1},{4,6},{6,4},{5,7},{7,5},{8,10},{10,8},{9,1... | collective-permute-start | bytes 2359304 | tf_op jit(solution)/shard_map/ppermute | solution.py:29
  461.2 14.4 %all-to-all-start.6 = ((f32[32,1,1536]{2,1,0:T(1,128)}), f32[32,1,1536]{2,1,0:T(1,128)}, u32[]{:S(2)}, u32[]{:S(2)}) async-start(f32[32,1,1536]{2,1,0:T(1,128)} %broadcast_in_dim.5), calls=%async_computation.7 | async-start | bytes 393216 | tf_op jit(solution)/shard_map/all_to_all | solution.py:1045
  (103 other events, 728.9 us)
Sparse Core Ops, SparseCore 0:
  265.1 115.4 reduce-scatter.1
